TPU v7x, 256 devices: a whole 4x4x8 slice. The times are simulated.
256 devices in a mesh: head: 8 (over z), tok: 32 (over x, y, core).
Axes of the slice: x: 4, y: 4, z: 8, core: 2. Of those that a mesh axis runs over, the one named last changes fastest.
Arguments:
- video_q: bfloat16 [28672, 2048], P('tok', 'head'), may hold values from -6 to 6
- video_k: bfloat16 [28672, 2048], P('tok', 'head'), may hold values from -6 to 6
- video_v: bfloat16 [28672, 2048], P('tok', 'head'), may hold values from -6 to 6
- audio_q: bfloat16 [1024, 2048], P('tok', 'head'), may hold values from -6 to 6
- audio_k: bfloat16 [1024, 2048], P('tok', 'head'), may hold values from -6 to 6
- audio_v: bfloat16 [1024, 2048], P('tok', 'head'), may hold values from -6 to 6
- norm_gain: float32 [2048], replicated, may hold values from 0.5 to 1.5
Outputs:
- video_out: bfloat16 [28672, 2048], P(('tok', 'head'))
- audio_out: bfloat16 [1024, 2048], P('tok', 'head')
All inputs are finite; a program needn't handle non-finite values.
Results may differ from a plain program's by a relative error of at most 0.0095.
Values may be sent and summed in bfloat16 or wider, within the bound.
A program may use at most 64 MiB of HBM per device.

v0:
```python
import jax
import jax.numpy as jnp
from jax import lax
from jax.sharding import PartitionSpec as P

HEAD_DIM = 64


def shards(video_q, video_k, video_v, audio_q, audio_k, audio_v, norm_gain):
    query_rows, local_width = video_q.shape
    heads_here = local_width // HEAD_DIM
    audio_rows = audio_q.shape[0]
    scaling = HEAD_DIM ** (-0.5)

    def split_heads(matrix):
        return matrix.reshape(matrix.shape[0], heads_here, HEAD_DIM)

    video_heads = split_heads(video_q)
    pieces = (
        lax.all_gather(audio_k, "tok", axis=0, tiled=True),
        lax.all_gather(audio_v, "tok", axis=0, tiled=True),
    )
    running_max = jnp.full((heads_here, query_rows), -1e30, jnp.float32)
    running_sum = jnp.zeros((heads_here, query_rows), jnp.float32)
    running_out = jnp.zeros((heads_here, query_rows, HEAD_DIM), jnp.float32)
    key_block = split_heads(pieces[0])
    value_block = split_heads(pieces[1])
    max_list = []
    sum_list = []
    out_list = []
    for absorb_head_index in range(heads_here):
        absorb_scores = (
            jnp.einsum(
                "qd,kd->qk",
                video_heads[:, absorb_head_index],
                key_block[:, absorb_head_index],
                preferred_element_type=jnp.float32,
            )
            * scaling
        )
        new_max = jnp.maximum(running_max[absorb_head_index], jnp.max(absorb_scores, axis=1))
        absorb_weights = jnp.exp(absorb_scores - new_max[:, None])
        factor = jnp.exp(running_max[absorb_head_index] - new_max)
        sum_list.append(running_sum[absorb_head_index] * factor + jnp.sum(absorb_weights, axis=1))
        out_list.append(
            running_out[absorb_head_index] * factor[:, None]
            + jnp.dot(
                absorb_weights.astype(jnp.bfloat16),
                value_block[:, absorb_head_index],
                preferred_element_type=jnp.float32,
            )
        )
        max_list.append(new_max)
    final_sum = jnp.stack(sum_list)
    final_out = jnp.stack(out_list)
    video_attn = (
        (final_out / final_sum[:, :, None]).transpose(1, 0, 2).reshape(query_rows, local_width)
    )
    video_attn = video_attn.astype(jnp.bfloat16)
    head_count = lax.axis_size("head")
    pieces = video_attn.reshape(head_count, query_rows // head_count, local_width)
    received = lax.all_to_all(pieces, "head", split_axis=0, concat_axis=2, tiled=True)
    normalize_received = received[0]
    widened = normalize_received.astype(jnp.float32)
    mean_square = jnp.mean(widened * widened, axis=-1, keepdims=True)
    video_out = (widened * lax.rsqrt(mean_square + 1e-06) * norm_gain).astype(jnp.bfloat16)
    all_queries = split_heads(lax.all_gather(audio_q, "tok", axis=0, tiled=True))
    video_keys = split_heads(video_k)
    video_values = split_heads(video_v)
    max_list, sum_list, out_list = ([], [], [])
    for head_index in range(heads_here):
        scores = (
            jnp.einsum(
                "qd,kd->qk",
                all_queries[:, head_index],
                video_keys[:, head_index],
                preferred_element_type=jnp.float32,
            )
            * scaling
        )
        local_max = jnp.max(scores, axis=1)
        weights = jnp.exp(scores - local_max[:, None])
        max_list.append(local_max)
        sum_list.append(jnp.sum(weights, axis=1))
        out_list.append(
            jnp.dot(
                weights.astype(jnp.bfloat16),
                video_values[:, head_index],
                preferred_element_type=jnp.float32,
            )
        )
    part_max = jnp.stack(max_list)
    part_sum = jnp.stack(sum_list)
    part_out = jnp.stack(out_list)
    tok_count = lax.axis_size("tok")
    grouped_max = part_max.reshape(heads_here, tok_count, audio_rows)
    grouped_sum = part_sum.reshape(heads_here, tok_count, audio_rows)
    grouped_out = part_out.reshape(heads_here, tok_count, audio_rows, HEAD_DIM)
    got_max, got_sum, got_out = (
        lax.all_to_all(grouped_max, "tok", split_axis=1, concat_axis=1, tiled=True),
        lax.all_to_all(grouped_sum, "tok", split_axis=1, concat_axis=1, tiled=True),
        lax.all_to_all(grouped_out, "tok", split_axis=1, concat_axis=1, tiled=True),
    )
    joint_max = jnp.max(got_max, axis=1, keepdims=True)
    factor = jnp.exp(got_max - joint_max)
    own_sum = jnp.sum(got_sum * factor, axis=1)
    own_out = jnp.sum(got_out * factor[:, :, :, None], axis=1)
    audio_out = (own_out / own_sum[:, :, None]).transpose(1, 0, 2).reshape(audio_rows, local_width)
    return (video_out, audio_out.astype(jnp.bfloat16))


def solution(mesh):
    placed = (
        P("tok", "head"),
        P("tok", "head"),
        P("tok", "head"),
        P("tok", "head"),
        P("tok", "head"),
        P("tok", "head"),
        P(),
    )
    return jax.shard_map(
        shards,
        mesh=mesh,
        in_specs=placed,
        out_specs=(P(("tok", "head"), None), P("tok", "head")),
        check_vma=False,
    )
```

profile of v0, /device:TPU:1, one launch (start us, length us, event | category | flops | bytes accessed | tf_op | source)
XLA Modules:
  0.0 200.3 jit_solution(15297851648713263094)
XLA Ops:
  0.6 1.3 copy.41
  1.9 26.4 %all_gather.11 = bf16[1024,256]{1,0:T(8,128)(2,1)S(1)} all-gather(bf16[32,256]{1,0:T(8,128)(2,1)} %param.10), channel_id=1, replica_groups=mesh['head'=8,'tok'=32] {'tok'}, dimensions={0}, use_global_device_ids=true | all-gather | bytes 540672 | tf_op jit(solution)/shard_map/all_gather | solution.py:67
  28.3 0.2 copy.40
  28.5 0.8 multiply_reduce_fusion
  29.3 2.5 %multiply_reduce_fusion.1 = (f32[1024]{0:T(1024)S(1)}, f32[1024,896]{1,0:T(8,128)}) fusion(bf16[896,4,64]{0,2,1:T(8,128)(2,1)S(1)} %bitcast.193, bf16[1024,4,64]{0,2,1:T(8,128)(2,1)S(1)} %bitcast.181), kind=kOutput, calls=%fused_computation.9 | convolution fusion | flops 119274496 | bytes 3919872 | tf_op jit(solution)/shard_map/qd,kd->qk/dot_general | solution.py:73
  31.8 2.6 %multiply_reduce_fusion.2 = (f32[1024]{0:T(1024)S(1)}, f32[1024,896]{1,0:T(8,128)}) fusion(bf16[896,4,64]{0,2,1:T(8,128)(2,1)S(1)} %bitcast.194, bf16[1024,4,64]{0,2,1:T(8,128)(2,1)S(1)} %bitcast.182), kind=kOutput, calls=%fused_computation.10 | convolution fusion | flops 119274496 | bytes 3919872 | tf_op jit(solution)/shard_map/qd,kd->qk/dot_general | solution.py:73
  34.4 2.5 %multiply_reduce_fusion.3 = (f32[1024]{0:T(1024)S(1)}, f32[1024,896]{1,0:T(8,128)}) fusion(bf16[896,4,64]{0,2,1:T(8,128)(2,1)S(1)} %bitcast.195, bf16[1024,4,64]{0,2,1:T(8,128)(2,1)S(1)} %bitcast.183), kind=kOutput, calls=%fused_computation.11 | convolution fusion | flops 119274496 | bytes 3919872 | tf_op jit(solution)/shard_map/qd,kd->qk/dot_general | solution.py:73
  36.9 2.0 fusion.14
  38.9 4.0 %fusion.12 = (f32[1024]{0:T(1024)S(1)}, bf16[1024,896]{1,0:T(8,128)(2,1)}) fusion(f32[1024,896]{1,0:T(8,128)} %get-tuple-element.31, f32[1024]{0:T(1024)S(1)} %get-tuple-element.30), kind=kLoop, calls=%fused_computation.28 | loop fusion | flops 3668992 | bytes 5513216 | tf_op jit(solution)/shard_map/reduce_sum | solution.py:84
  43.1 2.9 %fusion.10 = (f32[1024]{0:T(1024)S(1)}, bf16[1024,896]{1,0:T(8,128)(2,1)S(1)}) fusion(f32[1024,896]{1,0:T(8,128)} %get-tuple-element.33, f32[1024]{0:T(1024)S(1)} %get-tuple-element.32), kind=kLoop, calls=%fused_computation.26 | loop fusion | flops 3668992 | bytes 5513216 | tf_op jit(solution)/shard_map/reduce_sum | solution.py:84
  46.0 4.1 %fusion.8 = (f32[1024]{0:T(1024)S(1)}, bf16[1024,896]{1,0:T(8,128)(2,1)}) fusion(f32[1024,896]{1,0:T(8,128)} %get-tuple-element.35, f32[1024]{0:T(1024)S(1)} %get-tuple-element.34), kind=kLoop, calls=%fused_computation.24 | loop fusion | flops 3668992 | bytes 5513216 | tf_op jit(solution)/shard_map/reduce_sum | solution.py:84
  50.3 0.7 reshape.275
  51.0 5.1 %all-to-all-start.3 = ((f32[32,1,128]{2,1,0:T(1,128)}), f32[32,1,128]{2,1,0:T(1,128)S(1)}, u32[]{:S(2)}, u32[]{:S(2)}) async-start(f32[32,1,128]{2,1,0:T(1,128)} %reshape.275), calls=%async_computation.3 | async-start | bytes 32768 | tf_op jit(solution)/shard_map/all_to_all | solution.py:101
  56.2 0.2 copy.35
  56.4 25.3 %all_gather.9 = bf16[1024,256]{1,0:T(8,128)(2,1)S(1)} all-gather(bf16[32,256]{1,0:T(8,128)(2,1)S(1)} %copy-done.17), channel_id=1, replica_groups=mesh['head'=8,'tok'=32] {'tok'}, dimensions={0}, use_global_device_ids=true | all-gather | bytes 540672 | tf_op jit(solution)/shard_map/all_gather | solution.py:20
  81.8 0.2 copy.36
  82.0 3.1 %multiply_reduce_fusion.4 = (f32[896]{0:T(1024)}, f32[896,1024]{1,0:T(8,128)}) fusion(bf16[1024,4,64]{0,2,1:T(8,128)(2,1)S(1)} %bitcast.184, bf16[896,4,64]{0,2,1:T(8,128)(2,1)S(1)} %bitcast.196), kind=kOutput, calls=%fused_computation.12 | convolution fusion | flops 119274624 | bytes 3919360 | tf_op jit(solution)/shard_map/qd,kd->qk/dot_general | solution.py:33
  85.0 3.2 %multiply_reduce_fusion.5 = (f32[896]{0:T(1024)}, f32[896,1024]{1,0:T(8,128)}) fusion(bf16[1024,4,64]{0,2,1:T(8,128)(2,1)S(1)} %bitcast.185, bf16[896,4,64]{0,2,1:T(8,128)(2,1)S(1)} %bitcast.197), kind=kOutput, calls=%fused_computation.13 | convolution fusion | flops 119274624 | bytes 3919360 | tf_op jit(solution)/shard_map/qd,kd->qk/dot_general | solution.py:33
  88.2 3.1 %multiply_reduce_fusion.6 = (f32[896]{0:T(1024)}, f32[896,1024]{1,0:T(8,128)}) fusion(bf16[1024,4,64]{0,2,1:T(8,128)(2,1)S(1)} %bitcast.186, bf16[896,4,64]{0,2,1:T(8,128)(2,1)S(1)} %bitcast.198), kind=kOutput, calls=%fused_computation.14 | convolution fusion | flops 119274624 | bytes 3919360 | tf_op jit(solution)/shard_map/qd,kd->qk/dot_general | solution.py:33
  91.3 3.2 %multiply_reduce_fusion.7 = (f32[896]{0:T(1024)}, f32[896,1024]{1,0:T(8,128)}) fusion(bf16[1024,4,64]{0,2,1:T(8,128)(2,1)S(1)} %bitcast.187, bf16[896,4,64]{0,2,1:T(8,128)(2,1)S(1)} %bitcast.199), kind=kOutput, calls=%fused_computation.15 | convolution fusion | flops 119274624 | bytes 3919360 | tf_op jit(solution)/shard_map/qd,kd->qk/dot_general | solution.py:33
  94.5 0.7 stack.69
  95.2 0.7 stack.68
  95.8 0.7 stack.67
  96.5 0.7 stack.66
  97.2 0.2 copy.42
  97.5 24.1 %all_gather.10 = bf16[1024,256]{1,0:T(8,128)(2,1)S(1)} all-gather(bf16[32,256]{1,0:T(8,128)(2,1)} %param.12), channel_id=1, replica_groups=mesh['head'=8,'tok'=32] {'tok'}, dimensions={0}, use_global_device_ids=true | all-gather | bytes 540672 | tf_op jit(solution)/shard_map/all_gather | solution.py:21
  121.6 0.2 copy.37
  121.8 0.8 broadcast_maximum_fusion
  122.7 3.1 %fusion.6 = f32[896]{0:T(1024)S(1)} fusion(f32[896,1024]{1,0:T(8,128)} %get-tuple-element.21, f32[896]{0:T(1024)S(1)} %broadcast_maximum_fusion), kind=kLoop, calls=%fused_computation.22 | loop fusion | flops 2751616 | bytes 3677184 | tf_op jit(solution)/shard_map/reduce_sum | solution.py:44
  125.8 0.8 fusion.4
  126.7 0.8 fusion.36
  127.5 0.8 fusion.39
  128.4 0.3 copy-done.1
  128.7 0.8 fusion.2
  129.6 0.9 fusion.42
  130.5 0.3 copy-done
  130.8 0.8 fusion
  131.7 0.9 fusion.45
  132.5 0.6 convolution_bitcast_fusion
  133.2 0.8 fusion.50
  134.1 0.7 reshape.273
  134.8 4.5 %all-to-all-start.2 = ((f32[32,1,128]{2,1,0:T(1,128)}), f32[32,1,128]{2,1,0:T(1,128)S(1)}, u32[]{:S(2)}, u32[]{:S(2)}) async-start(f32[32,1,128]{2,1,0:T(1,128)} %reshape.273), calls=%async_computation.2 | async-start | bytes 32768 | tf_op jit(solution)/shard_map/all_to_all | solution.py:100
  139.3 2.9 %convolution_bitcast_fusion.1 = f32[1,32,32,64]{3,2,1,0:T(8,128)} fusion(bf16[32,32,896]{2,1,0:T(8,128)(2,1)} %bitcast.173, bf16[896,4,64]{0,2,1:T(8,128)(2,1)S(1)} %bitcast.189), kind=kOutput, calls=%fused_computation.39 | convolution fusion | flops 117440512 | bytes 2211840 | tf_op jit(solution)/shard_map/dot_general | solution.py:86
  142.2 1.6 convert_element_type.66
  143.8 1.1 copy.38
  144.9 1.2 all-to-all-done.2
  146.2 0.6 copy-done.7
  146.8 8.2 %all-to-all-start = ((bf16[8,112,256]{2,1,0:T(8,128)(2,1)}), bf16[8,112,256]{2,1,0:T(8,128)(2,1)S(1)}, u32[]{:S(2)}, u32[]{:S(2)}) async-start(bf16[8,112,256]{2,1,0:T(8,128)(2,1)} %copy.38), calls=%async_computation | async-start | bytes 917504 | tf_op jit(solution)/shard_map/all_to_all | solution.py:62
  155.0 0.6 convolution_bitcast_fusion.2
  155.6 2.1 %convolution_bitcast_fusion.3 = f32[1,32,32,64]{3,2,1,0:T(8,128)S(1)} fusion(bf16[32,32,896]{2,1,0:T(8,128)(2,1)} %bitcast.172, bf16[896,4,64]{0,2,1:T(8,128)(2,1)S(1)} %bitcast.191), kind=kOutput, calls=%fused_computation.41 | convolution fusion | flops 117440512 | bytes 2211840 | tf_op jit(solution)/shard_map/dot_general | solution.py:86
  157.7 1.3 copy_bitcast_fusion
  159.0 2.3 %reshape.271 = f32[32,1,8192]{2,1,0:T(1,128)} reshape(f32[32,4,32,64]{3,2,1,0:T(8,128)S(1)} %copy_bitcast_fusion) | data formatting | bytes 2097152
  161.3 0.6 broadcast.268
  161.9 0.7 reduce.3
  162.8 0.7 reduce.4
  163.7 7.7 %all-to-all-done = bf16[8,112,256]{2,1,0:T(8,128)(2,1)S(1)} async-done(((bf16[8,112,256]{2,1,0:T(8,128)(2,1)}), bf16[8,112,256]{2,1,0:T(8,128)(2,1)S(1)}, u32[]{:S(2)}, u32[]{:S(2)}) %all-to-all-start) | async-done | bytes 458784 | tf_op jit(solution)/shard_map/all_to_all | solution.py:62
  171.4 6.3 %all-to-all-start.1 = ((f32[32,1,8192]{2,1,0:T(1,128)}), f32[32,1,8192]{2,1,0:T(1,128)S(1)}, u32[]{:S(2)}, u32[]{:S(2)}) async-start(f32[32,1,8192]{2,1,0:T(1,128)} %reshape.271), calls=%async_computation.1 | async-start | bytes 2097152 | tf_op jit(solution)/shard_map/all_to_all | solution.py:102
  178.0 0.2 fusion.48
  178.2 0.9 multiply_convert_fusion
  179.1 15.6 %all-to-all-done.1 = f32[32,1,8192]{2,1,0:T(1,128)S(1)} async-done(((f32[32,1,8192]{2,1,0:T(1,128)}), f32[32,1,8192]{2,1,0:T(1,128)S(1)}, u32[]{:S(2)}, u32[]{:S(2)}) %all-to-all-start.1) | async-done | bytes 1048608 | tf_op jit(solution)/shard_map/all_to_all | solution.py:102
  194.7 3.3 %reduce.5 = f32[32,8192]{1,0:T(8,128)S(1)} reduce(f32[32,1,8192]{2,1,0:T(1,128)S(1)} %all-to-all-done.1, f32[]{:T(128)} %broadcast.268), dimensions={1}, to_apply=%all_to_all.17.reduce_sub_computation | reduce | bytes 2097156 | tf_op jit(solution)/shard_map/all_to_all | solution.py:102
  198.0 0.8 reshape.272
  198.8 0.7 multiply_reduce_fusion.8
  199.6 0.7 convert_element_type.78
  (63 shorter events, 1.2 us)
Async XLA Ops:
  45.9 10.2 %copy-start.5 = (bf16[896,256]{1,0:T(8,128)(2,1)S(1)}, bf16[896,256]{1,0:T(8,128)(2,1)}, u32[]{:S(2)}) copy-start(bf16[896,256]{1,0:T(8,128)(2,1)} %param.7) | copy-start | bytes 1376260
  45.9 10.5 %copy-start.17 = (bf16[32,256]{1,0:T(8,128)(2,1)S(1)}, bf16[32,256]{1,0:T(8,128)(2,1)}, u32[]{:S(2)}) copy-start(bf16[32,256]{1,0:T(8,128)(2,1)} %param.11) | copy-start | bytes 49156
  51.0 83.8 %all-to-all-start.3 = ((f32[32,1,128]{2,1,0:T(1,128)}), f32[32,1,128]{2,1,0:T(1,128)S(1)}, u32[]{:S(2)}, u32[]{:S(2)}) async-start(f32[32,1,128]{2,1,0:T(1,128)} %reshape.275), calls=%async_computation.3 | async-start | bytes 32768 | tf_op jit(solution)/shard_map/all_to_all | solution.py:101
  88.2 9.0 %copy-start.6 = (bf16[896,256]{1,0:T(8,128)(2,1)S(1)}, bf16[896,256]{1,0:T(8,128)(2,1)}, u32[]{:S(2)}) copy-start(bf16[896,256]{1,0:T(8,128)(2,1)} %param.9) | copy-start | bytes 1376260
  94.5 31.3 %copy-start.16 = (f32[896]{0:T(1024)S(1)}, f32[896]{0:T(1024)}, u32[]{:S(2)}) copy-start(f32[896]{0:T(1024)} %get-tuple-element.20) | copy-start | bytes 10756
  94.5 31.3 %copy-start.15 = (f32[896]{0:T(1024)S(1)}, f32[896]{0:T(1024)}, u32[]{:S(2)}) copy-start(f32[896]{0:T(1024)} %get-tuple-element.22) | copy-start | bytes 10756
  121.8 4.0 %copy-start.2 = (f32[896,1024]{1,0:T(8,128)S(1)}, f32[896,1024]{1,0:T(8,128)}, u32[]{:S(2)}) copy-start(f32[896,1024]{1,0:T(8,128)} %get-tuple-element.23) | copy-start | bytes 11010052
  122.7 4.0 %copy-start.3 = (f32[896,1024]{1,0:T(8,128)S(1)}, f32[896,1024]{1,0:T(8,128)}, u32[]{:S(2)}) copy-start(f32[896,1024]{1,0:T(8,128)} %get-tuple-element.21) | copy-start | bytes 11010052
  126.7 1.7 copy-start.14
  126.7 2.0 %copy-start.1 = (f32[896,1024]{1,0:T(8,128)S(1)}, f32[896,1024]{1,0:T(8,128)}, u32[]{:S(2)}) copy-start(f32[896,1024]{1,0:T(8,128)} %get-tuple-element.25) | copy-start | bytes 11010052
  128.7 1.7 copy-start.13
  128.7 2.0 %copy-start = (f32[896,1024]{1,0:T(8,128)S(1)}, f32[896,1024]{1,0:T(8,128)}, u32[]{:S(2)}) copy-start(f32[896,1024]{1,0:T(8,128)} %get-tuple-element.27) | copy-start | bytes 11010052
  130.8 1.8 copy-start.4
  131.6 2.4 %copy-start.9 = (f32[1,32,32]{2,0,1:T(1,128)S(1)}, f32[1,32,32]{2,0,1:T(1,128)}, u32[]{:S(2)}) copy-start(f32[1,32,32]{2,0,1:T(1,128)} %stack.69) | copy-start | bytes 12292
  131.6 2.4 %copy-start.10 = (f32[1,32,32]{2,0,1:T(1,128)S(1)}, f32[1,32,32]{2,0,1:T(1,128)}, u32[]{:S(2)}) copy-start(f32[1,32,32]{2,0,1:T(1,128)} %stack.68) | copy-start | bytes 12292
  131.6 2.4 %copy-start.11 = (f32[1,32,32]{2,0,1:T(1,128)S(1)}, f32[1,32,32]{2,0,1:T(1,128)}, u32[]{:S(2)}) copy-start(f32[1,32,32]{2,0,1:T(1,128)} %stack.67) | copy-start | bytes 12292
  131.6 2.4 %copy-start.12 = (f32[1,32,32]{2,0,1:T(1,128)S(1)}, f32[1,32,32]{2,0,1:T(1,128)}, u32[]{:S(2)}) copy-start(f32[1,32,32]{2,0,1:T(1,128)} %stack.66) | copy-start | bytes 12292
  134.8 11.4 %all-to-all-start.2 = ((f32[32,1,128]{2,1,0:T(1,128)}), f32[32,1,128]{2,1,0:T(1,128)S(1)}, u32[]{:S(2)}, u32[]{:S(2)}) async-start(f32[32,1,128]{2,1,0:T(1,128)} %reshape.273), calls=%async_computation.2 | async-start | bytes 32768 | tf_op jit(solution)/shard_map/all_to_all | solution.py:100
  146.2 0.6 copy-start.7
  146.8 24.6 %all-to-all-start = ((bf16[8,112,256]{2,1,0:T(8,128)(2,1)}), bf16[8,112,256]{2,1,0:T(8,128)(2,1)S(1)}, u32[]{:S(2)}, u32[]{:S(2)}) async-start(bf16[8,112,256]{2,1,0:T(8,128)(2,1)} %copy.38), calls=%async_computation | async-start | bytes 917504 | tf_op jit(solution)/shard_map/all_to_all | solution.py:62
  157.7 4.2 %copy-start.8 = (f32[32,1,128]{2,1,0:T(1,128)S(1)}, f32[32,1,128]{2,1,0:T(1,128)}, u32[]{:S(2)}) copy-start(f32[32,1,128]{2,1,0:T(1,128)} %copy-done.7) | copy-start | bytes 49156
  161.3 16.8 %copy-start.18 = (f32[2048]{0:T(1024)S(1)}, f32[2048]{0:T(1024)}, u32[]{:S(2)}) copy-start(f32[2048]{0:T(1024)} %param.13) | copy-start | bytes 24580
  171.4 23.3 %all-to-all-start.1 = ((f32[32,1,8192]{2,1,0:T(1,128)}), f32[32,1,8192]{2,1,0:T(1,128)S(1)}, u32[]{:S(2)}, u32[]{:S(2)}) async-start(f32[32,1,8192]{2,1,0:T(1,128)} %reshape.271), calls=%async_computation.1 | async-start | bytes 2097152 | tf_op jit(solution)/shard_map/all_to_all | solution.py:102
where the time goes:
time: 201 us; the launch traced here: 200 us
  blocking collectives  75.9 us (38%)
  matrix products  30.5 us (15%)
  other arithmetic  28.6 us (14%)
  waiting for transfers between devices  24.6 us (12%)
  starting transfers between devices  24.1 us (12%)
  local copies, waits for them, and re-layouts  15.6 us (8%)
    all_gather x1, blocking collectives, shards(): lax.all_gather(audio_q, 'tok', axis=0, tiled=True)  26.4 us
    all_gather x1, blocking collectives, shards(): lax.all_gather(audio_k, 'tok', axis=0, tiled=True)  25.3 us
    all_gather x1, blocking collectives, shards(): lax.all_gather(audio_v, 'tok', axis=0, tiled=True)  24.1 us
    all_to_all x1, waiting for transfers between devices, shards(): lax.all_to_all(grouped_out, 'tok', split_axis=1, concat_axis=1, tiled=True)  15.6 us
    reduce_sum x4, other arithmetic, shards(): sum_list.append(jnp.sum(weights, axis=1))  13 us
    dot_general x4, matrix products, shards(): jnp.einsum('qd,kd->qk', video_heads[:, absorb_head_index], key_block[:, a...  12.5 us
    dot_general x4, matrix products, shards(): jnp.einsum('qd,kd->qk', all_queries[:, head_index], video_keys[:, head_in...  8.31 us
    all_to_all x1, starting transfers between devices, shards(): lax.all_to_all(pieces, 'head', split_axis=0, concat_axis=2, tiled=True)  8.15 us
  transfers between devices with their start and end apart: 4, of which 3 were waited for; matrix products, arithmetic and copies ran while one was open for 22% of the time, Pallas kernels for 0%

commit v1 on v0

v1 whole, which is shorter than its diff:
```python
import jax
import jax.numpy as jnp
from jax import lax
from jax.experimental import pallas as pl
from jax.experimental.pallas import tpu as pltpu
from jax.sharding import PartitionSpec as P

MESH = pl.DeviceIdType.MESH
F32, BF16 = jnp.float32, jnp.bfloat16
HEAD_DIM = 64
LOG2E = 1.4426950408889634
NZ = 8
NT = 32
ROWS = 896
PIECE = 112
AROWS = 32
WIDTH = 256
KEYS = 1024
AUG = 80


def key_blocks(count):
    starts = list(range(0, count, 256))
    return [(start, min(256, count - start)) for start in starts]


def kernel(vq, vk, vv, aq, ak, av, gain, vout, aout,
           q_buf, k_buf, v_buf, qt, vt_local, kvg, qg, vt_audio, qt_audio,
           s_a, s_b, o_t, stage, recv, ret_stage, ret_recv, stat, stat_recv, w_buf,
           in_sem, kv_send, kv_recv, q_send, q_recv, fwd_send, fwd_recv,
           z_send, z_recv, ret_send, ret_rsem, st_send, st_rsem):
    z = lax.axis_index("head")
    t = lax.axis_index("tok")
    x, y, c = t // 8, (t // 2) % 4, t % 2

    def tok_of(dx, dy, dc):
        return (((x + dx) % 4) * 4 + (y + dy) % 4) * 2 + (c + dc) % 2

    own = [
        pltpu.make_async_copy(ak, kvg.at[0, 0], in_sem.at[0]),
        pltpu.make_async_copy(av, kvg.at[0, 1], in_sem.at[1]),
        pltpu.make_async_copy(aq, qg.at[0], in_sem.at[2]),
        pltpu.make_async_copy(vq, q_buf, in_sem.at[3]),
        pltpu.make_async_copy(vv, v_buf, in_sem.at[4]),
        pltpu.make_async_copy(vk, k_buf, in_sem.at[5]),
    ]
    for copy in own:
        copy.start()

    barrier = pltpu.get_barrier_semaphore()

    def greet_tok(b, carry):
        pl.semaphore_signal(barrier, inc=1, device_id=(z, tok_of(b // 4, b % 4, b // 16)),
                            device_id_type=MESH)
        return carry

    lax.fori_loop(1, NT, greet_tok, 0)

    def greet_head(d, carry):
        pl.semaphore_signal(barrier, inc=1, device_id=((z + d) % NZ, t), device_id_type=MESH)
        return carry

    lax.fori_loop(1, NZ, greet_head, 0)
    for copy in own[:3]:
        copy.wait()
    pl.semaphore_wait(barrier, NT - 1 + NZ - 1)

    def kv_copy(b):
        return pltpu.make_async_remote_copy(
            src_ref=kvg.at[0], dst_ref=kvg.at[b], send_sem=kv_send.at[b], recv_sem=kv_recv.at[b],
            device_id=(z, tok_of(4 - b // 4, 4 - b % 4, 0)), device_id_type=MESH)

    def q_copy(b):
        return pltpu.make_async_remote_copy(
            src_ref=qg.at[0], dst_ref=qg.at[b], send_sem=q_send.at[b], recv_sem=q_recv.at[b],
            device_id=(z, tok_of(4 - b // 4, 4 - b % 4, 0)), device_id_type=MESH)

    def loop(start, stop, body):
        def step(i, carry):
            body(i)
            return carry
        lax.fori_loop(start, stop, step, 0)

    loop(1, 16, lambda b: kv_copy(b).start())
    loop(1, 16, lambda b: q_copy(b).start())

    own[3].wait()
    for j in range(4):
        parts = []
        for d in (j + 1, (NZ - j) % NZ):
            start = pl.multiple_of(((z + d) % NZ) * PIECE, 16)
            parts.append(q_buf[pl.ds(start, PIECE), :])
            parts.append(jnp.zeros((128 - PIECE, WIDTH), BF16))
        qt[j] = jnp.concatenate(parts, axis=0).T * BF16(0.125)
    own[4].wait()
    for h in range(4):
        vt_local[h, HEAD_DIM:, :] = jnp.ones((AUG - HEAD_DIM, ROWS), BF16)
        vt_audio[h, HEAD_DIM:, :] = jnp.ones((AUG - HEAD_DIM, KEYS), BF16)
    for start, size in key_blocks(ROWS):
        turned = v_buf[start:start + size, :].T
        for h in range(4):
            vt_local[h, :HEAD_DIM, start:start + size] = turned[h * HEAD_DIM:(h + 1) * HEAD_DIM]
    own[5].wait()

    loop(1, 16, lambda b: kv_copy(b).wait_recv())
    sibling = (z, tok_of(0, 0, 1))
    kv_fwd = pltpu.make_async_remote_copy(
        src_ref=kvg.at[0:16], dst_ref=kvg.at[16:32], send_sem=fwd_send.at[0],
        recv_sem=fwd_recv.at[0], device_id=sibling, device_id_type=MESH)
    kv_fwd.start()
    q_fwd = pltpu.make_async_remote_copy(
        src_ref=qg.at[0:16], dst_ref=qg.at[16:32], send_sem=fwd_send.at[1],
        recv_sem=fwd_recv.at[1], device_id=sibling, device_id_type=MESH)

    def turn_values(half):
        for kb in (2 * half, 2 * half + 1):
            turned = kvg[8 * kb:8 * kb + 8, 1].reshape(256, WIDTH).T
            for h in range(4):
                vt_audio[h, :HEAD_DIM, kb * 256:kb * 256 + 256] = (
                    turned[h * HEAD_DIM:(h + 1) * HEAD_DIM])

    turn_values(0)
    kv_fwd.wait_recv()
    turn_values(1)

    row = lax.broadcasted_iota(jnp.int32, (128, 256), 0)

    def masked(qt_ref, j, h):
        pair = qt_ref[j, (h // 2) * 128:(h // 2) * 128 + 128, :]
        keep = (row < HEAD_DIM) if h % 2 == 0 else (row >= HEAD_DIM)
        return jnp.where(keep, pair, jnp.zeros_like(pair))

    def audio_keys(start, size, h):
        lanes = slice((h // 2) * 128, (h // 2) * 128 + 128)
        return kvg[start // 32:(start + size) // 32, 0, :, lanes].reshape(size, 128)

    def video_keys(start, size, h):
        return k_buf[start:start + size, (h // 2) * 128:(h // 2) * 128 + 128]

    def both(first, second):
        top, acc = None, None
        if first is not None:
            keys, count, qt_ref, j, h, s_out = first
            q_head = masked(qt_ref, j, h)
        if second is not None:
            s_in, top_in, vt_ref, h_in, count_in = second
        blocks = key_blocks(count if first is not None else count_in)
        for start, size in blocks:
            if first is not None:
                s = jnp.dot(keys(start, size, h), q_head, preferred_element_type=F32)
                s_out[start:start + size, :] = s
                part = jnp.max(s.reshape(size // 8, 8, 256), axis=0)
                top = part if top is None else jnp.maximum(top, part)
            if second is not None:
                w = jnp.exp2((s_in[start:start + size, :] - top_in) * LOG2E).astype(BF16)
                o = jnp.dot(vt_ref[h_in, :, start:start + size], w, preferred_element_type=F32)
                acc = o if acc is None else acc + o
        if top is not None:
            top = jnp.max(top, axis=0, keepdims=True)
        return top, acc

    def z_copy(d, slot):
        return pltpu.make_async_remote_copy(
            src_ref=stage.at[slot], dst_ref=recv.at[d], send_sem=z_send.at[d],
            recv_sem=z_recv.at[d], device_id=((z + d) % NZ, t), device_id_type=MESH)

    def slot_of(d):
        return 2 * (d - 1) if d <= 4 else 2 * (NZ - d) + 1

    def video_chunk(j, top):
        after = jnp.minimum(j + 1, 3)
        steps = [(0, j, s_a), (1, j, s_b), (2, j, s_a), (3, j, s_b), (0, after, s_a)]
        for h in range(4):
            nh, nj, ns = steps[h + 1]
            top, acc = both((audio_keys, KEYS, qt, nj, nh, ns), (steps[h][2], top, vt_audio, h, KEYS))
            o_t[h * HEAD_DIM:(h + 1) * HEAD_DIM, :] = acc[:HEAD_DIM] / acc[HEAD_DIM:HEAD_DIM + 1]
        out = o_t[...].T.astype(BF16)
        stage[2 * j] = out[:PIECE]
        stage[2 * j + 1] = out[128:128 + PIECE]
        z_copy(j + 1, 2 * j).start()

        @pl.when(j > 0)
        def _():
            z_copy(NZ - j, 2 * j + 1).start()

        @pl.when(j == 1)
        def _():
            loop(1, 16, lambda b: q_copy(b).wait_recv())
            q_fwd.start()
        return top

    top, _ = both((audio_keys, KEYS, qt, 0, 0, s_a), None)
    lax.fori_loop(0, 4, video_chunk, top)

    q_fwd.wait_recv()
    for j in range(4):
        qt_audio[j] = qg[8 * j:8 * j + 8].reshape(256, WIDTH).T * BF16(0.125)

    def ret_copies(b, half):
        device = (z, tok_of(b // 4, b % 4, b // 16))
        return (
            pltpu.make_async_remote_copy(
                src_ref=ret_stage.at[b], dst_ref=ret_recv.at[b], send_sem=ret_send.at[b],
                recv_sem=ret_rsem.at[b], device_id=device, device_id_type=MESH),
            pltpu.make_async_remote_copy(
                src_ref=stat.at[b // 8, half], dst_ref=stat_recv.at[b], send_sem=st_send.at[b],
                recv_sem=st_rsem.at[b], device_id=device, device_id_type=MESH))

    def audio_chunk(j, top):
        after = jnp.minimum(j + 1, 3)
        steps = [(0, j, s_a), (1, j, s_b), (2, j, s_a), (3, j, s_b), (0, after, s_a)]
        for h in range(4):
            nh, nj, ns = steps[h + 1]
            top_h = top
            top, acc = both((video_keys, ROWS, qt_audio, nj, nh, ns),
                            (steps[h][2], top_h, vt_local, h, ROWS))
            o_t[h * HEAD_DIM:(h + 1) * HEAD_DIM, :] = acc[:HEAD_DIM]
            for half in range(2):
                lanes = slice(half * 128, half * 128 + 128)
                stat[j, half, h:h + 1, :] = top_h[:, lanes]
                stat[j, half, 4 + h:5 + h, :] = acc[HEAD_DIM:HEAD_DIM + 1, lanes]
        out = o_t[...].T.astype(BF16).reshape(8, AROWS, WIDTH)
        for p in range(8):
            ret_stage[8 * j + p] = out[p]
        for p in range(8):
            def send(b=8 * j + p, half=p // 4):
                for copy in ret_copies(b, half):
                    copy.start()
            if p == 0:
                pl.when(j > 0)(send)
            else:
                send()
        return top

    top, _ = both((video_keys, ROWS, qt_audio, 0, 0, s_a), None)
    lax.fori_loop(0, 4, audio_chunk, top)

    for d in range(1, NZ):
        z_copy(d, slot_of(d)).wait_recv()

    def received(d):
        return (stage[1] if d == 0 else recv[d]).astype(F32)

    total = None
    for d in range(NZ):
        wide = received(d)
        part = jnp.sum(wide * wide, axis=1, keepdims=True)
        total = part if total is None else total + part
    factor = lax.rsqrt(total * (1.0 / (NZ * WIDTH)) + 1e-06)
    for d in range(NZ):
        column = pl.multiple_of(((z + NZ - d) % NZ) * WIDTH, WIDTH)
        lanes = pl.ds(column, WIDTH)
        vout[:, lanes] = (received(d) * factor * gain[:, lanes]).astype(BF16)

    def ret_wait(b):
        for copy in ret_copies(b, (b % 8) // 4):
            copy.wait_recv()

    loop(1, NT, ret_wait)
    tiles = []
    for b in range(NT):
        tile = stat[0, 0] if b == 0 else stat_recv[b]
        shift = (128 - 32 * (b % 4)) % 128
        tiles.append(pltpu.roll(tile, shift, 1) if shift else tile)
    peak = tiles[0]
    for tile in tiles[1:]:
        peak = jnp.maximum(peak, tile)
    norm = None
    weights = []
    for tile in tiles:
        w = jnp.exp2((tile - peak) * LOG2E)
        weights.append(w)
        part = w * pltpu.roll(tile, 4, 0)
        norm = part if norm is None else norm + part
    for b in range(NT):
        w_buf[b] = weights[b] / norm
    turned = w_buf[...].reshape(256, 128).T[:AROWS]
    lane = lax.broadcasted_iota(jnp.int32, (AROWS, 128), 1)
    merged = [None, None]
    for b in range(NT):
        for pair in range(2):
            at = b * 8 + 2 * pair
            w = jnp.where(lane < HEAD_DIM, turned[:, at:at + 1], turned[:, at + 1:at + 2])
            lanes = slice(pair * 128, pair * 128 + 128)
            part = w * (ret_stage[0, :, lanes] if b == 0 else ret_recv[b, :, lanes]).astype(F32)
            merged[pair] = part if merged[pair] is None else merged[pair] + part
    for pair in range(2):
        aout[:, pair * 128:pair * 128 + 128] = merged[pair].astype(BF16)

    def sent_gather(b):
        kv_copy(b).wait_send()
        q_copy(b).wait_send()

    loop(1, 16, sent_gather)
    kv_fwd.wait_send()
    q_fwd.wait_send()
    for d in range(1, NZ):
        z_copy(d, slot_of(d)).wait_send()

    def sent_back(b):
        for copy in ret_copies(b, (b % 8) // 4):
            copy.wait_send()

    loop(1, NT, sent_back)


def shards(video_q, video_k, video_v, audio_q, audio_k, audio_v, norm_gain):
    hbm = pl.BlockSpec(memory_space=pl.ANY)
    vmem = pl.BlockSpec(memory_space=pltpu.VMEM)
    dma = pltpu.SemaphoreType.DMA
    return pl.pallas_call(
        kernel,
        out_shape=(
            jax.ShapeDtypeStruct((PIECE, NZ * WIDTH), BF16),
            jax.ShapeDtypeStruct((AROWS, WIDTH), BF16),
        ),
        in_specs=[hbm] * 6 + [vmem],
        out_specs=(vmem, vmem),
        scratch_shapes=[
            pltpu.VMEM((ROWS, WIDTH), BF16),
            pltpu.VMEM((ROWS, WIDTH), BF16),
            pltpu.VMEM((ROWS, WIDTH), BF16),
            pltpu.VMEM((4, WIDTH, 256), BF16),
            pltpu.VMEM((4, AUG, ROWS), BF16),
            pltpu.VMEM((NT, 2, AROWS, WIDTH), BF16),
            pltpu.VMEM((NT, AROWS, WIDTH), BF16),
            pltpu.VMEM((4, AUG, KEYS), BF16),
            pltpu.VMEM((4, WIDTH, 256), BF16),
            pltpu.VMEM((KEYS, 256), F32),
            pltpu.VMEM((KEYS, 256), F32),
            pltpu.VMEM((WIDTH, 256), F32),
            pltpu.VMEM((NZ, PIECE, WIDTH), BF16),
            pltpu.VMEM((NZ, PIECE, WIDTH), BF16),
            pltpu.VMEM((NT, AROWS, WIDTH), BF16),
            pltpu.VMEM((NT, AROWS, WIDTH), BF16),
            pltpu.VMEM((4, 2, 8, 128), F32),
            pltpu.VMEM((NT, 8, 128), F32),
            pltpu.VMEM((NT, 8, 128), F32),
            dma((6,)), dma((16,)), dma((16,)), dma((16,)), dma((16,)), dma((2,)), dma((2,)),
            dma((NZ,)), dma((NZ,)), dma((NT,)), dma((NT,)), dma((NT,)), dma((NT,)),
        ],
        compiler_params=pltpu.CompilerParams(
            collective_id=0, has_side_effects=True, vmem_limit_bytes=40 * 1024 * 1024),
    )(video_q, video_k, video_v, audio_q, audio_k, audio_v, norm_gain.reshape(1, -1))


def solution(mesh):
    placed = P("tok", "head")
    return jax.shard_map(
        shards,
        mesh=mesh,
        in_specs=(placed,) * 6 + (P(),),
        out_specs=(P(("tok", "head"), None), placed),
        check_vma=False,
    )
```

time: 201 us -> 51.9 us (0.26)
  blocking collectives: 75.9 us -> 0 us
  Pallas kernels: 0 us -> 43.6 us
  matrix products: 30.5 us -> 0 us
  other arithmetic: 28.6 us -> 0 us
  waiting for transfers between devices: 24.6 us -> 0 us
  starting transfers between devices: 24.1 us -> 0 us
  local copies, waits for them, and re-layouts: 15.6 us -> 7.27 us
    all_gather x3 -> x0, blocking collectives: 75.9 us -> none  [the longest x1 26.4 us: shards(): lax.all_gather(audio_q, 'tok', axis=0, tiled=True)]
    pallas_call x0 -> x1, Pallas kernels: none -> 43.6 us  [shards(): pl.pallas_call(kernel, out_shape=(jax.ShapeDtypeStruct((PIECE, NZ * WIDTH...]
    dot_general x16 -> x0, matrix products: 30.5 us -> none  [the longest x4 12.5 us: shards(): jnp.einsum('qd,kd->qk', video_heads[:, absorb_head_index], key_block[:, a...]
    all_to_all x4 -> x0, waiting for transfers between devices: 24.6 us -> none  [the longest x1 15.6 us: shards(): lax.all_to_all(grouped_out, 'tok', split_axis=1, concat_axis=1, tiled=True)]
    all_to_all x4 -> x0, starting transfers between devices: 24.1 us -> none  [the longest x1 8.15 us: shards(): lax.all_to_all(pieces, 'head', split_axis=0, concat_axis=2, tiled=True)]
    reduce_sum x11 -> x0, other arithmetic: 19.5 us -> none  [the longest x4 13 us: shards(): sum_list.append(jnp.sum(weights, axis=1))]
    all_to_all x3 -> x0, other arithmetic: 4.72 us -> none  [the longest x1 3.26 us: shards(): lax.all_to_all(grouped_out, 'tok', split_axis=1, concat_axis=1, tiled=True)]
    convert_element_type x4 -> x0, local copies, waits for them, and re-layouts: 3.42 us -> none  [the longest x2 2.7 us: shards(): video_attn = video_attn.astype(jnp.bfloat16)]
  transfers between devices with their start and end apart: 4 -> 0, of which waited for: 3 -> 0; matrix products, arithmetic and copies ran while one was open for 22% -> 0% of each run, Pallas kernels for 0% -> 0%
where the time goes in v1:
time: 51.9 us; the launch traced here: 51.5 us
  Pallas kernels  43.6 us (84%)
  local copies, waits for them, and re-layouts  7.27 us (14%)
  between operations  0.66 us (1%)
    pallas_call x1, Pallas kernels, shards(): pl.pallas_call(kernel, out_shape=(jax.ShapeDtypeStruct((PIECE, NZ * WIDTH...  43.6 us
    unnamed x16, local copies, waits for them, and re-layouts  7.27 us

profile of v1, /device:TPU:1, one launch (start us, length us, event | category | flops | bytes accessed | tf_op | source)
XLA Modules:
  0.0 51.5 jit_solution(11126050596963837964)
XLA Ops:
  0.6 0.0 copy-start
  0.6 1.0 %copy-done = bf16[896,256]{1,0:T(8,128)(2,1)S(1)} copy-done((bf16[896,256]{1,0:T(8,128)(2,1)S(1)}, bf16[896,256]{1,0:T(8,128)(2,1)}, u32[]{:S(2)}) %copy-start) | copy-done | bytes 458776
  1.7 0.0 copy-start.1
  1.7 1.0 %copy-done.1 = bf16[896,256]{1,0:T(8,128)(2,1)S(1)} copy-done((bf16[896,256]{1,0:T(8,128)(2,1)S(1)}, bf16[896,256]{1,0:T(8,128)(2,1)}, u32[]{:S(2)}) %copy-start.1) | copy-done | bytes 458776
  2.7 0.0 copy-start.2
  2.7 1.0 %copy-done.2 = bf16[896,256]{1,0:T(8,128)(2,1)S(1)} copy-done((bf16[896,256]{1,0:T(8,128)(2,1)S(1)}, bf16[896,256]{1,0:T(8,128)(2,1)}, u32[]{:S(2)}) %copy-start.2) | copy-done | bytes 458776
  3.7 0.0 copy-start.3
  3.7 0.7 %copy-done.3 = bf16[32,256]{1,0:T(8,128)(2,1)S(1)} copy-done((bf16[32,256]{1,0:T(8,128)(2,1)S(1)}, bf16[32,256]{1,0:T(8,128)(2,1)}, u32[]{:S(2)}) %copy-start.3) | copy-done | bytes 16408
  4.4 0.0 copy-start.4
  4.4 0.7 %copy-done.4 = bf16[32,256]{1,0:T(8,128)(2,1)S(1)} copy-done((bf16[32,256]{1,0:T(8,128)(2,1)S(1)}, bf16[32,256]{1,0:T(8,128)(2,1)}, u32[]{:S(2)}) %copy-start.4) | copy-done | bytes 16408
  5.1 0.0 copy-start.5
  5.1 0.7 %copy-done.5 = bf16[32,256]{1,0:T(8,128)(2,1)S(1)} copy-done((bf16[32,256]{1,0:T(8,128)(2,1)S(1)}, bf16[32,256]{1,0:T(8,128)(2,1)}, u32[]{:S(2)}) %copy-start.5) | copy-done | bytes 16408
  5.8 0.0 copy-start.6
  5.8 0.7 %copy-done.6 = f32[2048]{0:T(1024)S(1)} copy-done((f32[2048]{0:T(1024)S(1)}, f32[2048]{0:T(1024)}, u32[]{:S(2)}) %copy-start.6) | copy-done | bytes 8216
  6.5 43.6 %shard_map.86 = (bf16[112,2048]{1,0:T(8,128)(2,1)S(1)}, bf16[32,256]{1,0:T(8,128)(2,1)S(1)}) custom-call(bf16[896,256]{1,0:T(8,128)(2,1)S(1)} %copy-done, bf16[896,256]{1,0:T(8,128)(2,1)S(1)} %copy-done.1, bf16[896,256]{1,0:T(8,128)(2,1)S(1)} %copy-done.2, bf16[32,256]{1,0:T(8,128)(2,1)S(1)} %copy-done.3, bf16[32,256]{1,0:T(8,128)(2,1)S(1)} %copy-done.4, ...), custom_call_target="tpu_custom_call" | custom-call | tf_op jit(solution)/shard_map/pallas_call | solution.py:311
  50.1 0.8 %copy.11 = bf16[112,2048]{1,0:T(8,128)(2,1)} copy(bf16[112,2048]{1,0:T(8,128)(2,1)S(1)} %get-tuple-element.4) | data formatting | bytes 917504
  50.9 0.6 %copy.12 = bf16[32,256]{1,0:T(8,128)(2,1)} copy(bf16[32,256]{1,0:T(8,128)(2,1)S(1)} %get-tuple-element.5) | data formatting | bytes 32768
Async XLA Ops:
  0.6 1.0 %copy-start = (bf16[896,256]{1,0:T(8,128)(2,1)S(1)}, bf16[896,256]{1,0:T(8,128)(2,1)}, u32[]{:S(2)}) copy-start(bf16[896,256]{1,0:T(8,128)(2,1)} %vq.1) | copy-start | bytes 1376260
  1.7 1.0 %copy-start.1 = (bf16[896,256]{1,0:T(8,128)(2,1)S(1)}, bf16[896,256]{1,0:T(8,128)(2,1)}, u32[]{:S(2)}) copy-start(bf16[896,256]{1,0:T(8,128)(2,1)} %vk.1) | copy-start | bytes 1376260
  2.7 1.0 %copy-start.2 = (bf16[896,256]{1,0:T(8,128)(2,1)S(1)}, bf16[896,256]{1,0:T(8,128)(2,1)}, u32[]{:S(2)}) copy-start(bf16[896,256]{1,0:T(8,128)(2,1)} %vv.1) | copy-start | bytes 1376260
  3.7 0.7 %copy-start.3 = (bf16[32,256]{1,0:T(8,128)(2,1)S(1)}, bf16[32,256]{1,0:T(8,128)(2,1)}, u32[]{:S(2)}) copy-start(bf16[32,256]{1,0:T(8,128)(2,1)} %aq.1) | copy-start | bytes 49156
  4.4 0.7 %copy-start.4 = (bf16[32,256]{1,0:T(8,128)(2,1)S(1)}, bf16[32,256]{1,0:T(8,128)(2,1)}, u32[]{:S(2)}) copy-start(bf16[32,256]{1,0:T(8,128)(2,1)} %ak.1) | copy-start | bytes 49156
  5.1 0.7 %copy-start.5 = (bf16[32,256]{1,0:T(8,128)(2,1)S(1)}, bf16[32,256]{1,0:T(8,128)(2,1)}, u32[]{:S(2)}) copy-start(bf16[32,256]{1,0:T(8,128)(2,1)} %av.1) | copy-start | bytes 49156
  5.8 0.7 %copy-start.6 = (f32[2048]{0:T(1024)S(1)}, f32[2048]{0:T(1024)}, u32[]{:S(2)}) copy-start(f32[2048]{0:T(1024)} %param.13) | copy-start | bytes 24580

commit v2 on v1

v2 whole, which is shorter than its diff:
```python
import jax
import jax.numpy as jnp
from jax import lax
from jax.experimental import pallas as pl
from jax.experimental.pallas import tpu as pltpu
from jax.sharding import PartitionSpec as P

MESH = pl.DeviceIdType.MESH
F32, BF16 = jnp.float32, jnp.bfloat16
HEAD_DIM = 64
LOG2E = 1.4426950408889634
NZ = 8
NC = 16
ROWS = 896
PIECE = 112
AROWS = 32
WIDTH = 256
KEYS = 1024
BLOCK = 512

CHIPS = sorted(((dx, dy) for dx in range(4) for dy in range(4)),
               key=lambda d: -(min(d[0], 4 - d[0]) + min(d[1], 4 - d[1])))
CHIPS = CHIPS[-1:] + CHIPS[:-1]


def key_blocks(count):
    return [(start, min(BLOCK, count - start)) for start in range(0, count, BLOCK)]


def slot_of(d):
    return 2 * (d - 4) if d >= 4 else 2 * (3 - d) + 1


def loop(start, stop, body):
    def step(i, carry):
        body(i)
        return carry
    lax.fori_loop(start, stop, step, 0)


def kernel(vq, vk, vv, aq, ak, av, gain_hbm, vout, aout,
           gain, q_buf, k_buf, v_buf, qt, vt_local, kvg, qg, vt_audio, qt_audio,
           s_a, s_b, o_t, stage, recv, pass_o, pass_st, got_o, got_st,
           ret_stage, ret_recv, stat, stat_recv, w_buf,
           in_sem, kv_send, kv_recv, q_send, q_recv, fwd_send, fwd_recv, qf_send, qf_recv,
           z_send, z_recv, po_send, po_recv, ps_send, ps_recv,
           ret_send, ret_rsem, st_send, st_rsem):
    z = lax.axis_index("head")
    t = lax.axis_index("tok")
    x, y, c = t // 8, (t // 2) % 4, t % 2
    xs = [((x + i) % 4) * 8 + c for i in range(4)]
    ys = [((y + i) % 4) * 2 for i in range(4)]
    zs = [(z + i) % NZ for i in range(NZ)]
    sibling = (z, t + 1 - 2 * c)

    def chip(s, sign=1):
        dx, dy = CHIPS[s]
        return (z, xs[sign * dx % 4] + ys[sign * dy % 4])

    own = [
        pltpu.make_async_copy(src, dst, in_sem.at[i]) for i, (src, dst) in enumerate([
            (ak, kvg.at[0, 0]), (av, kvg.at[0, 1]), (aq, qg.at[0]),
            (vq, q_buf), (vv, v_buf), (vk, k_buf), (gain_hbm, gain)])
    ]
    for copy in own:
        copy.start()

    barrier = pltpu.get_barrier_semaphore()

    def greet(device):
        pl.semaphore_signal(barrier, inc=1, device_id=device, device_id_type=MESH)

    for d in (4, 3, 5, 2, 6, 1, 7):
        greet((zs[d], t))
    for s in range(1, NC):
        greet(chip(s))
    greet(sibling)
    for copy in own[:3]:
        copy.wait()
    pl.semaphore_wait(barrier, NZ - 1 + NC)

    def kv_copy(s):
        return pltpu.make_async_remote_copy(
            src_ref=kvg.at[0], dst_ref=kvg.at[s], send_sem=kv_send.at[s], recv_sem=kv_recv.at[s],
            device_id=chip(s, -1), device_id_type=MESH)

    def q_copy(s):
        return pltpu.make_async_remote_copy(
            src_ref=qg.at[0], dst_ref=qg.at[s], send_sem=q_send.at[s], recv_sem=q_recv.at[s],
            device_id=chip(s, -1), device_id_type=MESH)

    for s in range(1, NC):
        kv_copy(s).start()
    for s in range(1, NC):
        q_copy(s).start()

    own[3].wait()
    for j in range(4):
        parts = []
        for d in (4 + j, 3 - j):
            start = pl.multiple_of(zs[d] * PIECE, 16)
            parts.append(q_buf[pl.ds(start, PIECE), :])
            parts.append(jnp.zeros((128 - PIECE, WIDTH), BF16))
        qt[j] = jnp.concatenate(parts, axis=0).T * BF16(0.125)
    own[4].wait()
    for start in range(0, ROWS, 128):
        turned = v_buf[start:start + 128, :].T
        for h in range(4):
            vt_local[h, :, start:start + 128] = turned[h * HEAD_DIM:(h + 1) * HEAD_DIM]
    own[5].wait()
    own[6].wait()

    def kv_fwd(g):
        return pltpu.make_async_remote_copy(
            src_ref=kvg.at[4 * g:4 * g + 4], dst_ref=kvg.at[NC + 4 * g:NC + 4 * g + 4],
            send_sem=fwd_send.at[g], recv_sem=fwd_recv.at[g], device_id=sibling, device_id_type=MESH)

    def turn_values(g):
        turned = kvg[4 * g:4 * g + 4, 1].reshape(128, WIDTH).T
        for h in range(4):
            vt_audio[h, :, g * 128:g * 128 + 128] = turned[h * HEAD_DIM:(h + 1) * HEAD_DIM]

    for g in range(4):
        for s in range(max(4 * g, 1), 4 * g + 4):
            kv_copy(s).wait_recv()
        kv_fwd(g).start()
        turn_values(g)
    for g in range(4):
        kv_fwd(g).wait_recv()
        turn_values(4 + g)

    q_fwd = pltpu.make_async_remote_copy(
        src_ref=qg.at[0:NC], dst_ref=qg.at[NC:2 * NC], send_sem=qf_send, recv_sem=qf_recv,
        device_id=sibling, device_id_type=MESH)

    row = lax.broadcasted_iota(jnp.int32, (128, 256), 0)

    def masked(qt_ref, j, h):
        pair = qt_ref[j, (h // 2) * 128:(h // 2) * 128 + 128, :]
        keep = (row < HEAD_DIM) if h % 2 == 0 else (row >= HEAD_DIM)
        return jnp.where(keep, pair, jnp.zeros_like(pair))

    def audio_keys(start, size, h):
        lanes = slice((h // 2) * 128, (h // 2) * 128 + 128)
        return kvg[start // 32:(start + size) // 32, 0, :, lanes].reshape(size, 128)

    def video_keys(start, size, h):
        return k_buf[start:start + size, (h // 2) * 128:(h // 2) * 128 + 128]

    def both(first, second):
        top, acc, total = None, None, None
        if first is not None:
            keys, count, qt_ref, j, h, s_out = first
            q_head = masked(qt_ref, j, h)
        if second is not None:
            s_in, top_in, vt_ref, h_in, count = second
        for start, size in key_blocks(count):
            if first is not None:
                s = jnp.dot(keys(start, size, h), q_head, preferred_element_type=F32)
                s_out[start:start + size, :] = s
                part = jnp.max(s.reshape(size // 8, 8, 256), axis=0)
                top = part if top is None else jnp.maximum(top, part)
            if second is not None:
                w = jnp.exp2((s_in[start:start + size, :] - top_in) * LOG2E)
                part = jnp.sum(w.reshape(size // 8, 8, 256), axis=0)
                total = part if total is None else total + part
                o = jnp.dot(vt_ref[h_in, :, start:start + size], w.astype(BF16),
                            preferred_element_type=F32)
                acc = o if acc is None else acc + o
        if top is not None:
            top = jnp.max(top, axis=0, keepdims=True)
        if total is not None:
            total = jnp.sum(total, axis=0, keepdims=True)
        return top, acc, total

    def z_copy(d, slot):
        return pltpu.make_async_remote_copy(
            src_ref=stage.at[slot], dst_ref=recv.at[d], send_sem=z_send.at[d],
            recv_sem=z_recv.at[d], device_id=((z + d) % NZ, t), device_id_type=MESH)

    def video_chunk(j, top):
        after = jnp.minimum(j + 1, 3)
        steps = [(0, j, s_a), (1, j, s_b), (2, j, s_a), (3, j, s_b), (0, after, s_a)]
        for h in range(4):
            nh, nj, ns = steps[h + 1]
            top, acc, total = both((audio_keys, KEYS, qt, nj, nh, ns),
                                   (steps[h][2], top, vt_audio, h, KEYS))
            o_t[h * HEAD_DIM:(h + 1) * HEAD_DIM, :] = acc / total
        out = o_t[...].T.astype(BF16)
        stage[2 * j] = out[:PIECE]
        stage[2 * j + 1] = out[128:128 + PIECE]
        z_copy(4 + j, 2 * j).start()

        @pl.when(j < 3)
        def _():
            z_copy(3 - j, 2 * j + 1).start()

        @pl.when(j == 1)
        def _():
            for s in range(1, NC):
                q_copy(s).wait_recv()
            q_fwd.start()
        return top

    top, _, _ = both((audio_keys, KEYS, qt, 0, 0, s_a), None)
    lax.fori_loop(0, 4, video_chunk, top)

    q_fwd.wait_recv()
    for j in range(4):
        qt_audio[j] = qg[8 * j:8 * j + 8].reshape(256, WIDTH).T * BF16(0.125)

    def pass_copies(j):
        return (
            pltpu.make_async_remote_copy(
                src_ref=pass_o.at[j], dst_ref=got_o.at[j], send_sem=po_send.at[j],
                recv_sem=po_recv.at[j], device_id=sibling, device_id_type=MESH),
            pltpu.make_async_remote_copy(
                src_ref=pass_st.at[j], dst_ref=got_st.at[j], send_sem=ps_send.at[j],
                recv_sem=ps_recv.at[j], device_id=sibling, device_id_type=MESH))

    def ret_copies(s, device):
        return (
            pltpu.make_async_remote_copy(
                src_ref=ret_stage.at[s], dst_ref=ret_recv.at[s], send_sem=ret_send.at[s],
                recv_sem=ret_rsem.at[s], device_id=device, device_id_type=MESH),
            pltpu.make_async_remote_copy(
                src_ref=stat.at[s // 4], dst_ref=stat_recv.at[s], send_sem=st_send.at[s],
                recv_sem=st_rsem.at[s], device_id=device, device_id_type=MESH))

    def audio_heads(j, after, top, finish):
        steps = [(0, j, s_a), (1, j, s_b), (2, j, s_a), (3, j, s_b), (0, after, s_a)]
        for h in range(4):
            nh, nj, ns = steps[h + 1]
            top_h = top
            top, acc, total = both((video_keys, ROWS, qt_audio, nj, nh, ns),
                                   (steps[h][2], top_h, vt_local, h, ROWS))
            finish(h, top_h, acc, total)
        return top

    def pass_chunk(j, top):
        def finish(h, top_h, acc, total):
            pass_o[j, h * HEAD_DIM:(h + 1) * HEAD_DIM, :] = acc.astype(BF16)
            pass_st[j, h:h + 1, :] = top_h
            pass_st[j, 4 + h:5 + h, :] = total

        top = audio_heads(2 + j, (3 + j) % 4, top, finish)
        for copy in pass_copies(j):
            copy.start()
        return top

    top, _, _ = both((video_keys, ROWS, qt_audio, 2, 0, s_a), None)
    top = lax.fori_loop(0, 2, pass_chunk, top)

    for j in range(2):
        for copy in pass_copies(j):
            copy.wait_recv()

        def finish(h, top_h, acc, total, j=j):
            other_top = got_st[j, h:h + 1, :]
            peak = jnp.maximum(top_h, other_top)
            a = jnp.exp2((top_h - peak) * LOG2E)
            b = jnp.exp2((other_top - peak) * LOG2E)
            rows = slice(h * HEAD_DIM, (h + 1) * HEAD_DIM)
            o_t[rows, :] = acc * a + got_o[j, rows, :].astype(F32) * b
            norm = total * a + got_st[j, 4 + h:5 + h, :] * b
            for half in range(2):
                lanes = slice(half * 128, half * 128 + 128)
                stat[2 * j + half, h:h + 1, :] = peak[:, lanes]
                stat[2 * j + half, 4 + h:5 + h, :] = norm[:, lanes]

        top = audio_heads(j, min(j + 1, 1), top, finish)
        out = o_t[...].T.astype(BF16).reshape(8, AROWS, WIDTH)
        for p in range(8):
            s = 8 * j + p
            ret_stage[s] = out[p]
        for s in range(8 * j, 8 * j + 8):
            if s > 0:
                for copy in ret_copies(s, chip(s)):
                    copy.start()

    for d in range(1, NZ):
        z_copy(d, slot_of(d)).wait_recv()

    def received(d):
        return (stage[slot_of(0)] if d == 0 else recv[d]).astype(F32)

    total = None
    for d in range(NZ):
        wide = received(d)
        part = jnp.sum(wide * wide, axis=1, keepdims=True)
        total = part if total is None else total + part
    factor = lax.rsqrt(total * (1.0 / (NZ * WIDTH)) + 1e-06)
    for d in range(NZ):
        column = pl.multiple_of(((z + NZ - d) % NZ) * WIDTH, WIDTH)
        lanes = pl.ds(column, WIDTH)
        vout[:, lanes] = (received(d) * factor * gain[:, lanes]).astype(BF16)

    for s in range(1, NC):
        for copy in ret_copies(s, chip(s)):
            copy.wait_recv()
    tiles = []
    for s in range(NC):
        tile = stat[0] if s == 0 else stat_recv[s]
        shift = (128 - 32 * (s % 4)) % 128
        tiles.append(pltpu.roll(tile, shift, 1) if shift else tile)
    peak = tiles[0]
    for tile in tiles[1:]:
        peak = jnp.maximum(peak, tile)
    norm = None
    weights = []
    for tile in tiles:
        w = jnp.exp2((tile - peak) * LOG2E)
        weights.append(w)
        part = w * pltpu.roll(tile, 4, 0)
        norm = part if norm is None else norm + part
    for s in range(NC):
        w_buf[s] = weights[s] / norm
    turned = w_buf[...].reshape(NC * 8, 128).T[:AROWS]
    lane = lax.broadcasted_iota(jnp.int32, (AROWS, 128), 1)
    for pair in range(2):
        lanes = slice(pair * 128, pair * 128 + 128)
        merged = None
        for s in range(NC):
            at = s * 8 + 2 * pair
            w = jnp.where(lane < HEAD_DIM, turned[:, at:at + 1], turned[:, at + 1:at + 2])
            part = w * (ret_stage[0, :, lanes] if s == 0 else ret_recv[s, :, lanes]).astype(F32)
            merged = part if merged is None else merged + part
        aout[:, lanes] = merged.astype(BF16)

    for s in range(1, NC):
        kv_copy(s).wait_send()
        q_copy(s).wait_send()
    for g in range(4):
        kv_fwd(g).wait_send()
    q_fwd.wait_send()
    for d in range(1, NZ):
        z_copy(d, slot_of(d)).wait_send()
    for j in range(2):
        for copy in pass_copies(j):
            copy.wait_send()
    for s in range(1, NC):
        for copy in ret_copies(s, chip(s)):
            copy.wait_send()


def shards(video_q, video_k, video_v, audio_q, audio_k, audio_v, norm_gain):
    arrays = (video_q, video_k, video_v, audio_q, audio_k, audio_v, norm_gain.reshape(1, -1))
    arrays = [pltpu.with_memory_space_constraint(a, pltpu.HBM) for a in arrays]
    vmem = pl.BlockSpec(memory_space=pltpu.VMEM)
    dma = pltpu.SemaphoreType.DMA
    return pl.pallas_call(
        kernel,
        out_shape=(
            jax.ShapeDtypeStruct((PIECE, NZ * WIDTH), BF16),
            jax.ShapeDtypeStruct((AROWS, WIDTH), BF16),
        ),
        in_specs=[pl.BlockSpec(memory_space=pltpu.HBM)] * 7,
        out_specs=(vmem, vmem),
        scratch_shapes=[
            pltpu.VMEM((1, NZ * WIDTH), F32),
            pltpu.VMEM((ROWS, WIDTH), BF16),
            pltpu.VMEM((ROWS, WIDTH), BF16),
            pltpu.VMEM((ROWS, WIDTH), BF16),
            pltpu.VMEM((4, WIDTH, 256), BF16),
            pltpu.VMEM((4, HEAD_DIM, ROWS), BF16),
            pltpu.VMEM((2 * NC, 2, AROWS, WIDTH), BF16),
            pltpu.VMEM((2 * NC, AROWS, WIDTH), BF16),
            pltpu.VMEM((4, HEAD_DIM, KEYS), BF16),
            pltpu.VMEM((4, WIDTH, 256), BF16),
            pltpu.VMEM((KEYS, 256), F32),
            pltpu.VMEM((KEYS, 256), F32),
            pltpu.VMEM((WIDTH, 256), F32),
            pltpu.VMEM((NZ, PIECE, WIDTH), BF16),
            pltpu.VMEM((NZ, PIECE, WIDTH), BF16),
            pltpu.VMEM((2, WIDTH, 256), BF16),
            pltpu.VMEM((2, 8, 256), F32),
            pltpu.VMEM((2, WIDTH, 256), BF16),
            pltpu.VMEM((2, 8, 256), F32),
            pltpu.VMEM((NC, AROWS, WIDTH), BF16),
            pltpu.VMEM((NC, AROWS, WIDTH), BF16),
            pltpu.VMEM((4, 8, 128), F32),
            pltpu.VMEM((NC, 8, 128), F32),
            pltpu.VMEM((NC, 8, 128), F32),
            dma((7,)), dma((NC,)), dma((NC,)), dma((NC,)), dma((NC,)), dma((4,)), dma((4,)),
            dma, dma, dma((NZ,)), dma((NZ,)), dma((2,)), dma((2,)), dma((2,)), dma((2,)),
            dma((NC,)), dma((NC,)), dma((NC,)), dma((NC,)),
        ],
        compiler_params=pltpu.CompilerParams(
            collective_id=0, has_side_effects=True, vmem_limit_bytes=24 * 1024 * 1024),
    )(*arrays)


def solution(mesh):
    placed = P("tok", "head")
    return jax.shard_map(
        shards,
        mesh=mesh,
        in_specs=(placed,) * 6 + (P(),),
        out_specs=(P(("tok", "head"), None), placed),
        check_vma=False,
    )
```

time: 51.9 us -> 40.7 us (0.78)
  local copies, waits for them, and re-layouts: 7.27 us -> 1.37 us
  Pallas kernels: 43.6 us -> 38.5 us
    unnamed x16 -> x2, local copies, waits for them, and re-layouts: 7.27 us -> 1.37 us
    pallas_call x1, Pallas kernels: 43.6 us -> 38.5 us  [shards(): pl.pallas_call(kernel, out_shape=(jax.ShapeDtypeStruct((PIECE, NZ * WIDTH...]
where the time goes in v2:
time: 40.7 us; the launch traced here: 40.5 us
  Pallas kernels  38.5 us (95%)
  local copies, waits for them, and re-layouts  1.37 us (3%)
  between operations  0.64 us (2%)
    pallas_call x1, Pallas kernels, shards(): pl.pallas_call(kernel, out_shape=(jax.ShapeDtypeStruct((PIECE, NZ * WIDTH...  38.5 us
    unnamed x2, local copies, waits for them, and re-layouts  1.37 us

profile of v2, /device:TPU:1, one launch (start us, length us, event | category | flops | bytes accessed | tf_op | source)
XLA Modules:
  0.0 40.5 jit_solution(17171558781600286723)
XLA Ops:
  0.6 38.5 %shard_map.86 = (bf16[112,2048]{1,0:T(8,128)(2,1)S(1)}, bf16[32,256]{1,0:T(8,128)(2,1)S(1)}) custom-call(bf16[896,256]{1,0:T(8,128)(2,1)} %vq.1, bf16[896,256]{1,0:T(8,128)(2,1)} %vk.1, bf16[896,256]{1,0:T(8,128)(2,1)} %vv.1, bf16[32,256]{1,0:T(8,128)(2,1)} %aq.1, bf16[32,256]{1,0:T(8,128)(2,1)} %ak.1, bf16[32,256]{1,0:T(8,128)(2,1)} %av.1, f32[1,2048]{1,0:T(1,128)} %bitcast.1), custom_call_target="tpu_custom_call" | custom-call | tf_op jit(solution)/shard_map/pallas_call | solution.py:351
  39.1 0.8 %copy.11 = bf16[112,2048]{1,0:T(8,128)(2,1)} copy(bf16[112,2048]{1,0:T(8,128)(2,1)S(1)} %get-tuple-element.4) | data formatting | bytes 917504
  39.9 0.6 %copy.12 = bf16[32,256]{1,0:T(8,128)(2,1)} copy(bf16[32,256]{1,0:T(8,128)(2,1)S(1)} %get-tuple-element.5) | data formatting | bytes 32768

commit v3 on v2

--- a/solution.py
+++ b/solution.py
@@ -17,6 +17,7 @@
 WIDTH = 256
 KEYS = 1024
 BLOCK = 512
+BEFORE = 3
 
 CHIPS = sorted(((dx, dy) for dx in range(4) for dy in range(4)),
                key=lambda d: -(min(d[0], 4 - d[0]) + min(d[1], 4 - d[1])))
@@ -28,7 +29,9 @@
 
 
 def slot_of(d):
-    return 2 * (d - 4) if d >= 4 else 2 * (3 - d) + 1
+    if d == 0:
+        return 1
+    return 2 * (4 - d) if d <= 4 else 2 * (d - 4) + 1
 
 
 def loop(start, stop, body):
@@ -38,10 +41,10 @@
     lax.fori_loop(start, stop, step, 0)
 
 
-def kernel(vq, vk, vv, aq, ak, av, gain_hbm, vout, aout,
+def kernel(vq, vk, vv, aq, ak, av, gain_hbm, vout, ret_recv, stat_recv,
            gain, q_buf, k_buf, v_buf, qt, vt_local, kvg, qg, vt_audio, qt_audio,
-           s_a, s_b, o_t, stage, recv, pass_o, pass_st, got_o, got_st,
-           ret_stage, ret_recv, stat, stat_recv, w_buf,
+           s_a, s_b, s_c, s_d, o_t, stage, recv, pass_o, pass_st, got_o, got_st,
+           ret_stage, stat,
            in_sem, kv_send, kv_recv, q_send, q_recv, fwd_send, fwd_recv, qf_send, qf_recv,
            z_send, z_recv, po_send, po_recv, ps_send, ps_recv,
            ret_send, ret_rsem, st_send, st_rsem):
@@ -57,77 +60,81 @@
         dx, dy = CHIPS[s]
         return (z, xs[sign * dx % 4] + ys[sign * dy % 4])
 
+    barrier = pltpu.get_barrier_semaphore()
+    peers = [(min(d, NZ - d), (zs[d], t)) for d in range(1, NZ)]
+    peers += [(min(CHIPS[i][0], 4 - CHIPS[i][0]) + min(CHIPS[i][1], 4 - CHIPS[i][1]), chip(i))
+              for i in range(1, NC)]
+    for _, device in sorted(peers, key=lambda peer: -peer[0]) + [(0, sibling)]:
+        pl.semaphore_signal(barrier, inc=1, device_id=device, device_id_type=MESH)
+
     own = [
         pltpu.make_async_copy(src, dst, in_sem.at[i]) for i, (src, dst) in enumerate([
-            (ak, kvg.at[0, 0]), (av, kvg.at[0, 1]), (aq, qg.at[0]),
-            (vq, q_buf), (vv, v_buf), (vk, k_buf), (gain_hbm, gain)])
+            (ak.at[:, 0:128], kvg.at[0, 0, 0]), (av.at[:, 0:128], kvg.at[0, 0, 1]),
+            (ak.at[:, 128:256], kvg.at[1, 0, 0]), (av.at[:, 128:256], kvg.at[1, 0, 1]),
+            (aq, qg.at[0]), (vq, q_buf), (vv, v_buf), (vk, k_buf), (gain_hbm, gain)])
     ]
     for copy in own:
         copy.start()
 
-    barrier = pltpu.get_barrier_semaphore()
-
-    def greet(device):
-        pl.semaphore_signal(barrier, inc=1, device_id=device, device_id_type=MESH)
-
-    for d in (4, 3, 5, 2, 6, 1, 7):
-        greet((zs[d], t))
-    for s in range(1, NC):
-        greet(chip(s))
-    greet(sibling)
-    for copy in own[:3]:
+    for copy in own[:5]:
         copy.wait()
     pl.semaphore_wait(barrier, NZ - 1 + NC)
 
-    def kv_copy(s):
+    def kv_copy(pair, s):
         return pltpu.make_async_remote_copy(
-            src_ref=kvg.at[0], dst_ref=kvg.at[s], send_sem=kv_send.at[s], recv_sem=kv_recv.at[s],
-            device_id=chip(s, -1), device_id_type=MESH)
+            src_ref=kvg.at[pair, 0], dst_ref=kvg.at[pair, s], send_sem=kv_send.at[pair, s],
+            recv_sem=kv_recv.at[pair, s], device_id=chip(s, -1), device_id_type=MESH)
 
     def q_copy(s):
         return pltpu.make_async_remote_copy(
             src_ref=qg.at[0], dst_ref=qg.at[s], send_sem=q_send.at[s], recv_sem=q_recv.at[s],
             device_id=chip(s, -1), device_id_type=MESH)
 
-    for s in range(1, NC):
-        kv_copy(s).start()
+    for pair in range(2):
+        for s in range(1, NC):
+            kv_copy(pair, s).start()
     for s in range(1, NC):
         q_copy(s).start()
 
-    own[3].wait()
+    own[5].wait()
     for j in range(4):
         parts = []
-        for d in (4 + j, 3 - j):
+        for d in (4 - j, 4 + j if j else 0):
             start = pl.multiple_of(zs[d] * PIECE, 16)
             parts.append(q_buf[pl.ds(start, PIECE), :])
             parts.append(jnp.zeros((128 - PIECE, WIDTH), BF16))
         qt[j] = jnp.concatenate(parts, axis=0).T * BF16(0.125)
-    own[4].wait()
+    own[6].wait()
     for start in range(0, ROWS, 128):
         turned = v_buf[start:start + 128, :].T
         for h in range(4):
             vt_local[h, :, start:start + 128] = turned[h * HEAD_DIM:(h + 1) * HEAD_DIM]
-    own[5].wait()
-    own[6].wait()
-
-    def kv_fwd(g):
+    own[7].wait()
+    own[8].wait()
+
+    def kv_fwd(pair, g):
         return pltpu.make_async_remote_copy(
-            src_ref=kvg.at[4 * g:4 * g + 4], dst_ref=kvg.at[NC + 4 * g:NC + 4 * g + 4],
-            send_sem=fwd_send.at[g], recv_sem=fwd_recv.at[g], device_id=sibling, device_id_type=MESH)
-
-    def turn_values(g):
-        turned = kvg[4 * g:4 * g + 4, 1].reshape(128, WIDTH).T
-        for h in range(4):
-            vt_audio[h, :, g * 128:g * 128 + 128] = turned[h * HEAD_DIM:(h + 1) * HEAD_DIM]
-
+            src_ref=kvg.at[pair, 4 * g:4 * g + 4], dst_ref=kvg.at[pair, NC + 4 * g:NC + 4 * g + 4],
+            send_sem=fwd_send.at[pair, g], recv_sem=fwd_recv.at[pair, g], device_id=sibling,
+            device_id_type=MESH)
+
+    def turn_values(pair, g):
+        turned = kvg[pair, 4 * g:4 * g + 4, 1].reshape(128, 128).T
+        for h in range(2):
+            vt_audio[2 * pair + h, :, g * 128:g * 128 + 128] = turned[h * HEAD_DIM:(h + 1) * HEAD_DIM]
+
+    def pass_on(pair):
+        for g in range(4):
+            for s in range(max(4 * g, 1), 4 * g + 4):
+                kv_copy(pair, s).wait_recv()
+            kv_fwd(pair, g).start()
+
+    pass_on(0)
     for g in range(4):
-        for s in range(max(4 * g, 1), 4 * g + 4):
-            kv_copy(s).wait_recv()
-        kv_fwd(g).start()
-        turn_values(g)
+        turn_values(0, g)
     for g in range(4):
-        kv_fwd(g).wait_recv()
-        turn_values(4 + g)
+        kv_fwd(0, g).wait_recv()
+        turn_values(0, 4 + g)
 
     q_fwd = pltpu.make_async_remote_copy(
         src_ref=qg.at[0:NC], dst_ref=qg.at[NC:2 * NC], send_sem=qf_send, recv_sem=qf_recv,
@@ -141,8 +148,7 @@
         return jnp.where(keep, pair, jnp.zeros_like(pair))
 
     def audio_keys(start, size, h):
-        lanes = slice((h // 2) * 128, (h // 2) * 128 + 128)
-        return kvg[start // 32:(start + size) // 32, 0, :, lanes].reshape(size, 128)
+        return kvg[h // 2, start // 32:(start + size) // 32, 0].reshape(size, 128)
 
     def video_keys(start, size, h):
         return k_buf[start:start + size, (h // 2) * 128:(h // 2) * 128 + 128]
@@ -173,37 +179,48 @@
             total = jnp.sum(total, axis=0, keepdims=True)
         return top, acc, total
 
-    def z_copy(d, slot):
+    def z_copy(pair, d, slot):
         return pltpu.make_async_remote_copy(
-            src_ref=stage.at[slot], dst_ref=recv.at[d], send_sem=z_send.at[d],
-            recv_sem=z_recv.at[d], device_id=((z + d) % NZ, t), device_id_type=MESH)
-
-    def video_chunk(j, top):
+            src_ref=stage.at[pair, slot], dst_ref=recv.at[pair, d], send_sem=z_send.at[pair, d],
+            recv_sem=z_recv.at[pair, d], device_id=((z + d) % NZ, t), device_id_type=MESH)
+
+    def video_chunk(pair, at_one, j, top):
         after = jnp.minimum(j + 1, 3)
-        steps = [(0, j, s_a), (1, j, s_b), (2, j, s_a), (3, j, s_b), (0, after, s_a)]
-        for h in range(4):
-            nh, nj, ns = steps[h + 1]
-            top, acc, total = both((audio_keys, KEYS, qt, nj, nh, ns),
-                                   (steps[h][2], top, vt_audio, h, KEYS))
-            o_t[h * HEAD_DIM:(h + 1) * HEAD_DIM, :] = acc / total
-        out = o_t[...].T.astype(BF16)
-        stage[2 * j] = out[:PIECE]
-        stage[2 * j + 1] = out[128:128 + PIECE]
-        z_copy(4 + j, 2 * j).start()
-
-        @pl.when(j < 3)
+        h0, h1 = 2 * pair, 2 * pair + 1
+        top, acc, total = both((audio_keys, KEYS, qt, j, h1, s_b), (s_a, top, vt_audio, h0, KEYS))
+        o_t[:HEAD_DIM, :] = acc / total
+        top, acc, total = both((audio_keys, KEYS, qt, after, h0, s_a), (s_b, top, vt_audio, h1, KEYS))
+        o_t[HEAD_DIM:2 * HEAD_DIM, :] = acc / total
+        out = o_t[:2 * HEAD_DIM, :].T.astype(BF16)
+        stage[pair, 2 * j] = out[:PIECE]
+        stage[pair, 2 * j + 1] = out[128:128 + PIECE]
+        z_copy(pair, 4 - j, 2 * j).start()
+
+        @pl.when(j > 0)
         def _():
-            z_copy(3 - j, 2 * j + 1).start()
-
-        @pl.when(j == 1)
-        def _():
-            for s in range(1, NC):
-                q_copy(s).wait_recv()
-            q_fwd.start()
+            z_copy(pair, 4 + j, 2 * j + 1).start()
+
+        pl.when(j == 1 - pair)(at_one)
         return top
 
-    top, _, _ = both((audio_keys, KEYS, qt, 0, 0, s_a), None)
-    lax.fori_loop(0, 4, video_chunk, top)
+    def video_start(pair):
+        return both((audio_keys, KEYS, qt, 0, 2 * pair, s_a), None)[0]
+
+    def video_chunks(pair, start, stop, at_one, top):
+        return lax.fori_loop(start, stop, lambda j, top: video_chunk(pair, at_one, j, top), top)
+
+    def pass_queries():
+        for s in range(1, NC):
+            q_copy(s).wait_recv()
+        q_fwd.start()
+
+    video_chunks(0, 0, 4, lambda: pass_on(1), video_start(0))
+    for g in range(4):
+        turn_values(1, g)
+    for g in range(4):
+        kv_fwd(1, g).wait_recv()
+        turn_values(1, 4 + g)
+    video_top = video_chunks(1, 0, BEFORE, pass_queries, video_start(1))
 
     q_fwd.wait_recv()
     for j in range(4):
@@ -228,7 +245,7 @@
                 recv_sem=st_rsem.at[s], device_id=device, device_id_type=MESH))
 
     def audio_heads(j, after, top, finish):
-        steps = [(0, j, s_a), (1, j, s_b), (2, j, s_a), (3, j, s_b), (0, after, s_a)]
+        steps = [(0, j, s_c), (1, j, s_d), (2, j, s_c), (3, j, s_d), (0, after, s_c)]
         for h in range(4):
             nh, nj, ns = steps[h + 1]
             top_h = top
@@ -248,7 +265,7 @@
             copy.start()
         return top
 
-    top, _, _ = both((video_keys, ROWS, qt_audio, 2, 0, s_a), None)
+    top, _, _ = both((video_keys, ROWS, qt_audio, 2, 0, s_c), None)
     top = lax.fori_loop(0, 2, pass_chunk, top)
 
     for j in range(2):
@@ -277,30 +294,60 @@
             if s > 0:
                 for copy in ret_copies(s, chip(s)):
                     copy.start()
-
-    for d in range(1, NZ):
-        z_copy(d, slot_of(d)).wait_recv()
-
-    def received(d):
-        return (stage[slot_of(0)] if d == 0 else recv[d]).astype(F32)
+    if BEFORE < 4:
+        video_chunks(1, BEFORE, 4, pass_queries, video_top)
+    ret_recv[0] = ret_stage[0]
+    stat_recv[0] = stat[0]
+
+    for pair in range(2):
+        for d in range(1, NZ):
+            z_copy(pair, d, slot_of(d)).wait_recv()
+
+    def received(pair, d):
+        return (stage[pair, slot_of(0)] if d == 0 else recv[pair, d]).astype(F32)
 
     total = None
-    for d in range(NZ):
-        wide = received(d)
-        part = jnp.sum(wide * wide, axis=1, keepdims=True)
-        total = part if total is None else total + part
+    for pair in range(2):
+        for d in range(NZ):
+            wide = received(pair, d)
+            part = jnp.sum(wide * wide, axis=1, keepdims=True)
+            total = part if total is None else total + part
     factor = lax.rsqrt(total * (1.0 / (NZ * WIDTH)) + 1e-06)
     for d in range(NZ):
-        column = pl.multiple_of(((z + NZ - d) % NZ) * WIDTH, WIDTH)
-        lanes = pl.ds(column, WIDTH)
-        vout[:, lanes] = (received(d) * factor * gain[:, lanes]).astype(BF16)
+        for pair in range(2):
+            column = pl.multiple_of(((z + NZ - d) % NZ) * WIDTH + 128 * pair, 128)
+            lanes = pl.ds(column, 128)
+            vout[:, lanes] = (received(pair, d) * factor * gain[:, lanes]).astype(BF16)
 
     for s in range(1, NC):
         for copy in ret_copies(s, chip(s)):
             copy.wait_recv()
+
+    for s in range(1, NC):
+        kv_copy(0, s).wait_send()
+        kv_copy(1, s).wait_send()
+        q_copy(s).wait_send()
+    for g in range(4):
+        kv_fwd(0, g).wait_send()
+        kv_fwd(1, g).wait_send()
+    q_fwd.wait_send()
+    for d in range(1, NZ):
+        z_copy(0, d, slot_of(d)).wait_send()
+        z_copy(1, d, slot_of(d)).wait_send()
+    for j in range(2):
+        for copy in pass_copies(j):
+            copy.wait_send()
+    for s in range(1, NC):
+        for copy in ret_copies(s, chip(s)):
+            copy.wait_send()
+
+
+def finish_kernel(rows, ret_recv, stat_recv, vout, aout, merged_buf, w_buf, sem):
+    rows_out = pltpu.make_async_copy(rows, vout, sem.at[0])
+    rows_out.start()
     tiles = []
     for s in range(NC):
-        tile = stat[0] if s == 0 else stat_recv[s]
+        tile = stat_recv[s]
         shift = (128 - 32 * (s % 4)) % 128
         tiles.append(pltpu.roll(tile, shift, 1) if shift else tile)
     peak = tiles[0]
@@ -323,24 +370,13 @@
         for s in range(NC):
             at = s * 8 + 2 * pair
             w = jnp.where(lane < HEAD_DIM, turned[:, at:at + 1], turned[:, at + 1:at + 2])
-            part = w * (ret_stage[0, :, lanes] if s == 0 else ret_recv[s, :, lanes]).astype(F32)
+            part = w * ret_recv[s, :, lanes].astype(F32)
             merged = part if merged is None else merged + part
-        aout[:, lanes] = merged.astype(BF16)
-
-    for s in range(1, NC):
-        kv_copy(s).wait_send()
-        q_copy(s).wait_send()
-    for g in range(4):
-        kv_fwd(g).wait_send()
-    q_fwd.wait_send()
-    for d in range(1, NZ):
-        z_copy(d, slot_of(d)).wait_send()
-    for j in range(2):
-        for copy in pass_copies(j):
-            copy.wait_send()
-    for s in range(1, NC):
-        for copy in ret_copies(s, chip(s)):
-            copy.wait_send()
+        merged_buf[:, lanes] = merged.astype(BF16)
+    merged_out = pltpu.make_async_copy(merged_buf, aout, sem.at[1])
+    merged_out.start()
+    merged_out.wait()
+    rows_out.wait()
 
 
 def shards(video_q, video_k, video_v, audio_q, audio_k, audio_v, norm_gain):
@@ -348,14 +384,15 @@
     arrays = [pltpu.with_memory_space_constraint(a, pltpu.HBM) for a in arrays]
     vmem = pl.BlockSpec(memory_space=pltpu.VMEM)
     dma = pltpu.SemaphoreType.DMA
-    return pl.pallas_call(
+    rows, ret_recv, stat_recv = pl.pallas_call(
         kernel,
         out_shape=(
             jax.ShapeDtypeStruct((PIECE, NZ * WIDTH), BF16),
-            jax.ShapeDtypeStruct((AROWS, WIDTH), BF16),
+            jax.ShapeDtypeStruct((NC, AROWS, WIDTH), BF16),
+            jax.ShapeDtypeStruct((NC, 8, 128), F32),
         ),
         in_specs=[pl.BlockSpec(memory_space=pltpu.HBM)] * 7,
-        out_specs=(vmem, vmem),
+        out_specs=(vmem, vmem, vmem),
         scratch_shapes=[
             pltpu.VMEM((1, NZ * WIDTH), F32),
             pltpu.VMEM((ROWS, WIDTH), BF16),
@@ -363,31 +400,45 @@
             pltpu.VMEM((ROWS, WIDTH), BF16),
             pltpu.VMEM((4, WIDTH, 256), BF16),
             pltpu.VMEM((4, HEAD_DIM, ROWS), BF16),
-            pltpu.VMEM((2 * NC, 2, AROWS, WIDTH), BF16),
+            pltpu.VMEM((2, 2 * NC, 2, AROWS, 128), BF16),
             pltpu.VMEM((2 * NC, AROWS, WIDTH), BF16),
             pltpu.VMEM((4, HEAD_DIM, KEYS), BF16),
             pltpu.VMEM((4, WIDTH, 256), BF16),
             pltpu.VMEM((KEYS, 256), F32),
             pltpu.VMEM((KEYS, 256), F32),
+            pltpu.VMEM((ROWS, 256), F32),
+            pltpu.VMEM((ROWS, 256), F32),
             pltpu.VMEM((WIDTH, 256), F32),
-            pltpu.VMEM((NZ, PIECE, WIDTH), BF16),
-            pltpu.VMEM((NZ, PIECE, WIDTH), BF16),
+            pltpu.VMEM((2, NZ, PIECE, 128), BF16),
+            pltpu.VMEM((2, NZ, PIECE, 128), BF16),
             pltpu.VMEM((2, WIDTH, 256), BF16),
             pltpu.VMEM((2, 8, 256), F32),
             pltpu.VMEM((2, WIDTH, 256), BF16),
             pltpu.VMEM((2, 8, 256), F32),
             pltpu.VMEM((NC, AROWS, WIDTH), BF16),
-            pltpu.VMEM((NC, AROWS, WIDTH), BF16),
             pltpu.VMEM((4, 8, 128), F32),
-            pltpu.VMEM((NC, 8, 128), F32),
-            pltpu.VMEM((NC, 8, 128), F32),
-            dma((7,)), dma((NC,)), dma((NC,)), dma((NC,)), dma((NC,)), dma((4,)), dma((4,)),
-            dma, dma, dma((NZ,)), dma((NZ,)), dma((2,)), dma((2,)), dma((2,)), dma((2,)),
+            dma((9,)), dma((2, NC)), dma((2, NC)), dma((NC,)), dma((NC,)), dma((2, 4)), dma((2, 4)),
+            dma, dma, dma((2, NZ)), dma((2, NZ)), dma((2,)), dma((2,)), dma((2,)), dma((2,)),
             dma((NC,)), dma((NC,)), dma((NC,)), dma((NC,)),
         ],
         compiler_params=pltpu.CompilerParams(
             collective_id=0, has_side_effects=True, vmem_limit_bytes=24 * 1024 * 1024),
     )(*arrays)
+    return pl.pallas_call(
+        finish_kernel,
+        out_shape=(
+            jax.ShapeDtypeStruct((PIECE, NZ * WIDTH), BF16),
+            jax.ShapeDtypeStruct((AROWS, WIDTH), BF16),
+        ),
+        in_specs=[vmem] * 3,
+        out_specs=(pl.BlockSpec(memory_space=pltpu.HBM),) * 2,
+        scratch_shapes=[
+            pltpu.VMEM((AROWS, WIDTH), BF16),
+            pltpu.VMEM((NC, 8, 128), F32),
+            dma((2,)),
+        ],
+        compiler_params=pltpu.CompilerParams(vmem_limit_bytes=4 * 1024 * 1024),
+    )(rows, ret_recv, stat_recv)
 
 
 def solution(mesh):

time: 40.7 us -> 39 us (0.958)
  local copies, waits for them, and re-layouts: 1.37 us -> 0 us
    pallas_call x1, Pallas kernels: 38.5 us -> 36.9 us  [shards(): pl.pallas_call(kernel, out_shape=(jax.ShapeDtypeStruct((PIECE, NZ * WIDTH...]
    unnamed x2 -> x0, local copies, waits for them, and re-layouts: 1.37 us -> none
    pallas_call x0 -> x1, Pallas kernels: none -> 1.31 us  [shards(): pl.pallas_call(finish_kernel, out_shape=(jax.ShapeDtypeStruct((PIECE, NZ...]
where the time goes in v3:
time: 39 us; the launch traced here: 38.9 us
  Pallas kernels  38.2 us (98%)
  between operations  0.64 us (2%)
    pallas_call x1, Pallas kernels, shards(): pl.pallas_call(kernel, out_shape=(jax.ShapeDtypeStruct((PIECE, NZ * WIDTH...  36.9 us
    pallas_call x1, Pallas kernels, shards(): pl.pallas_call(finish_kernel, out_shape=(jax.ShapeDtypeStruct((PIECE, NZ...  1.31 us

profile of v3, /device:TPU:1, one launch (start us, length us, event | category | flops | bytes accessed | tf_op | source)
XLA Modules:
  0.0 38.9 jit_solution(1156264341778813657)
XLA Ops:
  0.6 36.9 %shard_map.86 = (bf16[112,2048]{1,0:T(8,128)(2,1)S(1)}, bf16[16,32,256]{2,1,0:T(8,128)(2,1)S(1)}, f32[16,8,128]{2,1,0:T(8,128)S(1)}) custom-call(bf16[896,256]{1,0:T(8,128)(2,1)} %vq.1, bf16[896,256]{1,0:T(8,128)(2,1)} %vk.1, bf16[896,256]{1,0:T(8,128)(2,1)} %vv.1, bf16[32,256]{1,0:T(8,128)(2,1)} %aq.1, bf16[32,256]{1,0:T(8,128)(2,1)} %ak.1, ...), custom_call_target="tpu_custom_call" | custom-call | tf_op jit(solution)/shard_map/pallas_call | solution.py:387
  37.6 1.3 %shard_map.87 = (bf16[112,2048]{1,0:T(8,128)(2,1)}, bf16[32,256]{1,0:T(8,128)(2,1)}) custom-call(bf16[112,2048]{1,0:T(8,128)(2,1)S(1)} %get-tuple-element.5.rows, bf16[16,32,256]{2,1,0:T(8,128)(2,1)S(1)} %get-tuple-element.6.ret_recv, f32[16,8,128]{2,1,0:T(8,128)S(1)} %get-tuple-element.7.stat_recv), custom_call_target="tpu_custom_call" | custom-call | tf_op jit(solution)/shard_map/pallas_call | solution.py:427

commit v4 on v3

--- a/solution.py
+++ b/solution.py
@@ -17,7 +17,7 @@
 WIDTH = 256
 KEYS = 1024
 BLOCK = 512
-BEFORE = 3
+BEFORE = 2
 
 CHIPS = sorted(((dx, dy) for dx in range(4) for dy in range(4)),
                key=lambda d: -(min(d[0], 4 - d[0]) + min(d[1], 4 - d[1])))
@@ -90,11 +90,12 @@
             src_ref=qg.at[0], dst_ref=qg.at[s], send_sem=q_send.at[s], recv_sem=q_recv.at[s],
             device_id=chip(s, -1), device_id_type=MESH)
 
-    for pair in range(2):
-        for s in range(1, NC):
-            kv_copy(pair, s).start()
+    for s in range(1, NC):
+        kv_copy(0, s).start()
     for s in range(1, NC):
         q_copy(s).start()
+    for s in range(1, NC):
+        kv_copy(1, s).start()
 
     own[5].wait()
     for j in range(4):
@@ -200,7 +201,8 @@
         def _():
             z_copy(pair, 4 + j, 2 * j + 1).start()
 
-        pl.when(j == 1 - pair)(at_one)
+        if at_one is not None:
+            pl.when(j == 1)(at_one)
         return top
 
     def video_start(pair):
@@ -214,13 +216,7 @@
             q_copy(s).wait_recv()
         q_fwd.start()
 
-    video_chunks(0, 0, 4, lambda: pass_on(1), video_start(0))
-    for g in range(4):
-        turn_values(1, g)
-    for g in range(4):
-        kv_fwd(1, g).wait_recv()
-        turn_values(1, 4 + g)
-    video_top = video_chunks(1, 0, BEFORE, pass_queries, video_start(1))
+    video_chunks(0, 0, 4, pass_queries, video_start(0))
 
     q_fwd.wait_recv()
     for j in range(4):
@@ -249,7 +245,7 @@
         for h in range(4):
             nh, nj, ns = steps[h + 1]
             top_h = top
-            top, acc, total = both((video_keys, ROWS, qt_audio, nj, nh, ns),
+            top, acc, total = both((video_keys, ROWS, qt_audio, nj, nh, ns) if nj is not None else None,
                                    (steps[h][2], top_h, vt_local, h, ROWS))
             finish(h, top_h, acc, total)
         return top
@@ -263,10 +259,21 @@
         top = audio_heads(2 + j, (3 + j) % 4, top, finish)
         for copy in pass_copies(j):
             copy.start()
+
+        @pl.when(j == 0)
+        def _():
+            pass_on(1)
         return top
 
     top, _, _ = both((video_keys, ROWS, qt_audio, 2, 0, s_c), None)
     top = lax.fori_loop(0, 2, pass_chunk, top)
+
+    for g in range(4):
+        turn_values(1, g)
+    for g in range(4):
+        kv_fwd(1, g).wait_recv()
+        turn_values(1, 4 + g)
+    video_top = video_chunks(1, 0, BEFORE, None, video_start(1))
 
     for j in range(2):
         for copy in pass_copies(j):
@@ -285,7 +292,7 @@
                 stat[2 * j + half, h:h + 1, :] = peak[:, lanes]
                 stat[2 * j + half, 4 + h:5 + h, :] = norm[:, lanes]
 
-        top = audio_heads(j, min(j + 1, 1), top, finish)
+        top = audio_heads(j, 1 if j == 0 else None, top, finish)
         out = o_t[...].T.astype(BF16).reshape(8, AROWS, WIDTH)
         for p in range(8):
             s = 8 * j + p
@@ -295,7 +302,7 @@
                 for copy in ret_copies(s, chip(s)):
                     copy.start()
     if BEFORE < 4:
-        video_chunks(1, BEFORE, 4, pass_queries, video_top)
+        video_chunks(1, BEFORE, 4, None, video_top)
     ret_recv[0] = ret_stage[0]
     stat_recv[0] = stat[0]
 

time: 39 us -> 38.2 us (0.979)
  Pallas kernels: 38.2 us -> 37.5 us
    pallas_call x1, Pallas kernels: 36.9 us -> 36.2 us  [shards(): pl.pallas_call(kernel, out_shape=(jax.ShapeDtypeStruct((PIECE, NZ * WIDTH...]
where the time goes in v4:
time: 38.2 us; the launch traced here: 38.1 us
  Pallas kernels  37.5 us (98%)
  between operations  0.64 us (2%)
    pallas_call x1, Pallas kernels, shards(): pl.pallas_call(kernel, out_shape=(jax.ShapeDtypeStruct((PIECE, NZ * WIDTH...  36.2 us
    pallas_call x1, Pallas kernels, shards(): pl.pallas_call(finish_kernel, out_shape=(jax.ShapeDtypeStruct((PIECE, NZ...  1.31 us

profile of v4, /device:TPU:1, one launch (start us, length us, event | category | flops | bytes accessed | tf_op | source)
XLA Modules:
  0.0 38.1 jit_solution(11712610121545286035)
XLA Ops:
  0.6 36.2 %shard_map.86 = (bf16[112,2048]{1,0:T(8,128)(2,1)S(1)}, bf16[16,32,256]{2,1,0:T(8,128)(2,1)S(1)}, f32[16,8,128]{2,1,0:T(8,128)S(1)}) custom-call(bf16[896,256]{1,0:T(8,128)(2,1)} %vq.1, bf16[896,256]{1,0:T(8,128)(2,1)} %vk.1, bf16[896,256]{1,0:T(8,128)(2,1)} %vv.1, bf16[32,256]{1,0:T(8,128)(2,1)} %aq.1, bf16[32,256]{1,0:T(8,128)(2,1)} %ak.1, ...), custom_call_target="tpu_custom_call" | custom-call | tf_op jit(solution)/shard_map/pallas_call | solution.py:394
  36.8 1.3 %shard_map.87 = (bf16[112,2048]{1,0:T(8,128)(2,1)}, bf16[32,256]{1,0:T(8,128)(2,1)}) custom-call(bf16[112,2048]{1,0:T(8,128)(2,1)S(1)} %get-tuple-element.5.rows, bf16[16,32,256]{2,1,0:T(8,128)(2,1)S(1)} %get-tuple-element.6.ret_recv, f32[16,8,128]{2,1,0:T(8,128)S(1)} %get-tuple-element.7.stat_recv), custom_call_target="tpu_custom_call" | custom-call | tf_op jit(solution)/shard_map/pallas_call | solution.py:434

commit v5 on v4

--- a/solution.py
+++ b/solution.py
@@ -185,12 +185,13 @@
             src_ref=stage.at[pair, slot], dst_ref=recv.at[pair, d], send_sem=z_send.at[pair, d],
             recv_sem=z_recv.at[pair, d], device_id=((z + d) % NZ, t), device_id_type=MESH)
 
-    def video_chunk(pair, at_one, j, top):
+    def video_chunk(pair, at_one, j, top, last=False):
         after = jnp.minimum(j + 1, 3)
         h0, h1 = 2 * pair, 2 * pair + 1
         top, acc, total = both((audio_keys, KEYS, qt, j, h1, s_b), (s_a, top, vt_audio, h0, KEYS))
         o_t[:HEAD_DIM, :] = acc / total
-        top, acc, total = both((audio_keys, KEYS, qt, after, h0, s_a), (s_b, top, vt_audio, h1, KEYS))
+        top, acc, total = both(None if last else (audio_keys, KEYS, qt, after, h0, s_a),
+                               (s_b, top, vt_audio, h1, KEYS))
         o_t[HEAD_DIM:2 * HEAD_DIM, :] = acc / total
         out = o_t[:2 * HEAD_DIM, :].T.astype(BF16)
         stage[pair, 2 * j] = out[:PIECE]
@@ -209,7 +210,8 @@
         return both((audio_keys, KEYS, qt, 0, 2 * pair, s_a), None)[0]
 
     def video_chunks(pair, start, stop, at_one, top):
-        return lax.fori_loop(start, stop, lambda j, top: video_chunk(pair, at_one, j, top), top)
+        top = lax.fori_loop(start, min(stop, 3), lambda j, top: video_chunk(pair, at_one, j, top), top)
+        return video_chunk(pair, None, jnp.int32(3), top, last=True) if stop == 4 else top
 
     def pass_queries():
         for s in range(1, NC):
@@ -306,15 +308,13 @@
     ret_recv[0] = ret_stage[0]
     stat_recv[0] = stat[0]
 
+    def received(pair, d):
+        return (stage[pair, slot_of(0)] if d == 0 else recv[pair, d]).astype(F32)
+
+    total = None
     for pair in range(2):
         for d in range(1, NZ):
             z_copy(pair, d, slot_of(d)).wait_recv()
-
-    def received(pair, d):
-        return (stage[pair, slot_of(0)] if d == 0 else recv[pair, d]).astype(F32)
-
-    total = None
-    for pair in range(2):
         for d in range(NZ):
             wide = received(pair, d)
             part = jnp.sum(wide * wide, axis=1, keepdims=True)

time: 38.2 us -> 38.1 us (level)
  no operation moved by 1% of the time
where the time goes in v5:
time: 38.1 us; the launch traced here: 38 us
  Pallas kernels  37.4 us (98%)
  between operations  0.64 us (2%)
    pallas_call x1, Pallas kernels, shards(): pl.pallas_call(kernel, out_shape=(jax.ShapeDtypeStruct((PIECE, NZ * WIDTH...  36.1 us
    pallas_call x1, Pallas kernels, shards(): pl.pallas_call(finish_kernel, out_shape=(jax.ShapeDtypeStruct((PIECE, NZ...  1.31 us

profile of v5, /device:TPU:1, one launch (start us, length us, event | category | flops | bytes accessed | tf_op | source)
XLA Modules:
  0.0 38.0 jit_solution(17260623231920694698)
XLA Ops:
  0.6 36.1 %shard_map.86 = (bf16[112,2048]{1,0:T(8,128)(2,1)S(1)}, bf16[16,32,256]{2,1,0:T(8,128)(2,1)S(1)}, f32[16,8,128]{2,1,0:T(8,128)S(1)}) custom-call(bf16[896,256]{1,0:T(8,128)(2,1)} %vq.1, bf16[896,256]{1,0:T(8,128)(2,1)} %vk.1, bf16[896,256]{1,0:T(8,128)(2,1)} %vv.1, bf16[32,256]{1,0:T(8,128)(2,1)} %aq.1, bf16[32,256]{1,0:T(8,128)(2,1)} %ak.1, ...), custom_call_target="tpu_custom_call" | custom-call | tf_op jit(solution)/shard_map/pallas_call | solution.py:394
  36.7 1.3 %shard_map.87 = (bf16[112,2048]{1,0:T(8,128)(2,1)}, bf16[32,256]{1,0:T(8,128)(2,1)}) custom-call(bf16[112,2048]{1,0:T(8,128)(2,1)S(1)} %get-tuple-element.5.rows, bf16[16,32,256]{2,1,0:T(8,128)(2,1)S(1)} %get-tuple-element.6.ret_recv, f32[16,8,128]{2,1,0:T(8,128)S(1)} %get-tuple-element.7.stat_recv), custom_call_target="tpu_custom_call" | custom-call | tf_op jit(solution)/shard_map/pallas_call | solution.py:434

commit v6 on v5

--- a/solution.py
+++ b/solution.py
@@ -133,9 +133,6 @@
     pass_on(0)
     for g in range(4):
         turn_values(0, g)
-    for g in range(4):
-        kv_fwd(0, g).wait_recv()
-        turn_values(0, 4 + g)
 
     q_fwd = pltpu.make_async_remote_copy(
         src_ref=qg.at[0:NC], dst_ref=qg.at[NC:2 * NC], send_sem=qf_send, recv_sem=qf_recv,
@@ -207,7 +204,17 @@
         return top
 
     def video_start(pair):
-        return both((audio_keys, KEYS, qt, 0, 2 * pair, s_a), None)[0]
+        q_head = masked(qt, 0, 2 * pair)
+        tops = []
+        for start in (0, BLOCK):
+            if start:
+                for g in range(4):
+                    kv_fwd(pair, g).wait_recv()
+                    turn_values(pair, 4 + g)
+            s = jnp.dot(audio_keys(start, BLOCK, 2 * pair), q_head, preferred_element_type=F32)
+            s_a[start:start + BLOCK, :] = s
+            tops.append(jnp.max(s, axis=0, keepdims=True))
+        return jnp.maximum(*tops)
 
     def video_chunks(pair, start, stop, at_one, top):
         top = lax.fori_loop(start, min(stop, 3), lambda j, top: video_chunk(pair, at_one, j, top), top)
@@ -272,9 +279,6 @@
 
     for g in range(4):
         turn_values(1, g)
-    for g in range(4):
-        kv_fwd(1, g).wait_recv()
-        turn_values(1, 4 + g)
     video_top = video_chunks(1, 0, BEFORE, None, video_start(1))
 
     for j in range(2):

time: 38.1 us -> 38.4 us (level)
  no operation moved by 1% of the time
where the time goes in v6:
time: 38.4 us; the launch traced here: 38.3 us
  Pallas kernels  37.6 us (98%)
  between operations  0.64 us (2%)
    pallas_call x1, Pallas kernels, shards(): pl.pallas_call(kernel, out_shape=(jax.ShapeDtypeStruct((PIECE, NZ * WIDTH...  36.3 us
    pallas_call x1, Pallas kernels, shards(): pl.pallas_call(finish_kernel, out_shape=(jax.ShapeDtypeStruct((PIECE, NZ...  1.31 us

profile of v6, /device:TPU:1, one launch (start us, length us, event | category | flops | bytes accessed | tf_op | source)
XLA Modules:
  0.0 38.3 jit_solution(312764844360522716)
XLA Ops:
  0.6 36.3 %shard_map.86 = (bf16[112,2048]{1,0:T(8,128)(2,1)S(1)}, bf16[16,32,256]{2,1,0:T(8,128)(2,1)S(1)}, f32[16,8,128]{2,1,0:T(8,128)S(1)}) custom-call(bf16[896,256]{1,0:T(8,128)(2,1)} %vq.1, bf16[896,256]{1,0:T(8,128)(2,1)} %vk.1, bf16[896,256]{1,0:T(8,128)(2,1)} %vv.1, bf16[32,256]{1,0:T(8,128)(2,1)} %aq.1, bf16[32,256]{1,0:T(8,128)(2,1)} %ak.1, ...), custom_call_target="tpu_custom_call" | custom-call | tf_op jit(solution)/shard_map/pallas_call | solution.py:398
  37.0 1.3 %shard_map.87 = (bf16[112,2048]{1,0:T(8,128)(2,1)}, bf16[32,256]{1,0:T(8,128)(2,1)}) custom-call(bf16[112,2048]{1,0:T(8,128)(2,1)S(1)} %get-tuple-element.5.rows, bf16[16,32,256]{2,1,0:T(8,128)(2,1)S(1)} %get-tuple-element.6.ret_recv, f32[16,8,128]{2,1,0:T(8,128)S(1)} %get-tuple-element.7.stat_recv), custom_call_target="tpu_custom_call" | custom-call | tf_op jit(solution)/shard_map/pallas_call | solution.py:438
